TPU v7x, 32 devices: a whole 2x2x4 slice. The times are simulated.
32 devices in a mesh: day: 2 (over x), chan: 16 (over z, y, core).
Axes of the slice: x: 2, y: 2, z: 4, core: 2. Of those that a mesh axis runs over, the one named last changes fastest.
Arguments:
- records: bfloat16 [1024, 8, 3000], P(('day', 'chan')), parts along dimension 0, may hold values from -6 to 6
- live_mask: int32 [1024], P(('day', 'chan')), parts along dimension 0, may hold values 0 or 1
- offsets: int32 [16], replicated, may hold values from 1 to 511, as said below
Outputs:
- correlations: bfloat16 [1024, 16, 2048], P(('day', 'chan')), parts along dimension 0
There are 2 independent parts, one for each index of `day`. A program takes and returns all parts, laid end to end along the dimension named above; an argument that names none is the same for every part. Nothing has to cross between parts.
Inputs may be any that keep to these rules, and one draw needn't show every extreme that they name: offsets[k] lies between k * 32 + 1 and (k + 1) * 32, and the last one equals 511.
All inputs are finite; a program needn't handle non-finite values. No bound on the sum of `live_mask` on one device may be relied on, other than what follows from the above.
Results may differ from a plain program's by a relative error of at most 0.0076.
Values may be sent and summed in bfloat16 or wider, within the bound.
A program may use at most 128 MiB of HBM per device.

v0:
```python
import functools
import math

import jax
import jax.numpy as jnp
import numpy as np
from jax import lax
from jax.experimental import pallas as pl
from jax.experimental.pallas import tpu as pltpu
from jax.sharding import PartitionSpec as P

F = 512
F0 = 6
LAGS = 2048
LANES = 128
BAND = 512
PIECES = 4
LAYER_CHIPS = 4


def forward_table(length):
    samples = np.arange(length, dtype=np.int64)
    freqs = F0 + np.arange(F, dtype=np.int64)
    phase = np.mod(samples[:, None] * freqs[None, :], length)
    angle = 2.0 * math.pi / length * phase
    return np.concatenate([np.cos(angle), -np.sin(angle)], axis=1).astype(np.float32).astype(jnp.bfloat16)


def inverse_table(length):
    freqs = F0 + np.arange(F, dtype=np.int64)
    shifts = np.arange(LAGS, dtype=np.int64) - LAGS // 2
    phase = np.mod(freqs[:, None] * shifts[None, :], length)
    angle = 2.0 * math.pi / length * phase
    return np.concatenate([np.cos(angle), -np.sin(angle)], axis=0).astype(np.float32).astype(jnp.bfloat16)


def whiten(records, live_mask):
    count, windows, length = records.shape
    spectrum = jnp.dot(
        records.reshape(count * windows, length),
        jnp.asarray(forward_table(length)),
        preferred_element_type=jnp.float32,
    )
    power = jnp.mean(spectrum * spectrum, axis=1, keepdims=True)
    gain = jnp.repeat(live_mask.astype(jnp.float32), windows)[:, None]
    white = spectrum * (gain * lax.rsqrt(power + 1e-06))
    return white.astype(jnp.bfloat16)


def reach_kernel(shape, offsets_ref, white_ref, cross_ref, held, ext, own, swapped, made, back,
                 z_send, z_recv, c_send, c_recv, y_send, y_recv, d_send, d_recv, e_send, r_send, r_recv):
    layers, columns, depth, pieces, windows, fold = shape
    count, slab = white_ref.shape[0], white_ref.shape[1]
    pairs = offsets_ref.shape[0]
    wide = 2 * columns
    total = layers * wide * count
    me = lax.axis_index("chan")
    z, q = me // wide, me % wide
    y, c = q // 2, q % 2
    sibling = me + 1 - 2 * c
    sib_q = q + 1 - 2 * c
    mate = me + 2 - 4 * y
    mate_q = q + 2 - 4 * y
    far_q = sib_q + 2 - 4 * y
    step = count // pieces
    top, lifted = layers - 1, depth + 1

    barrier = pltpu.get_barrier_semaphore()

    def greet(device):
        pl.semaphore_signal(barrier, inc=1, device_id={"chan": device}, device_id_type=pl.DeviceIdType.MESH)

    greet(sibling)
    if columns == 2:
        greet(mate)

    @pl.when(z >= 1)
    def _():
        greet(me - wide)

    @pl.when(z < layers - 1)
    def _():
        greet(me + wide)

    below, above = jnp.minimum(z, 1), jnp.minimum(top - z, 1)
    peers = columns + below + above
    if fold:
        @pl.when(z == 0)
        def _():
            for i in range(wide):
                greet(top * wide + i)

        @pl.when(z == top)
        def _():
            for i in range(wide):
                greet(jnp.int32(i))

        peers = peers + wide * (2 - below - above)
    pl.semaphore_wait(barrier, peers)

    def rows(p):
        return pl.ds(p * step, step)

    def mine(dz, p):
        return white_ref.at[rows(p)] if dz == 0 else held.at[dz * wide + q, rows(p)]

    def copy(source, slot, p, send, recv, device):
        return pltpu.make_async_remote_copy(
            src_ref=source,
            dst_ref=held.at[slot, rows(p)],
            send_sem=send,
            recv_sem=recv,
            device_id={"chan": device},
            device_id_type=pl.DeviceIdType.MESH,
        )

    def down(dz, p):
        return copy(mine(dz, p), (dz + 1) * wide + q, p, z_send.at[dz, p], z_recv.at[dz + 1, p], me - wide)

    def from_above(dz, p):
        return copy(mine(dz, p), dz * wide + q, p, z_send.at[dz, p], z_recv.at[dz, p], me)

    def across(dz, p, slot):
        return copy(mine(dz, p), slot, p, c_send.at[dz, p], c_recv.at[dz, p], sibling)

    def over(dz, p, slot):
        return copy(mine(dz, p), slot, p, y_send.at[dz, p], y_recv.at[dz, p], mate)

    def onward(dz, p, slot):
        return copy(held.at[dz * wide + mate_q, rows(p)], slot, p, d_send.at[dz, p], d_recv.at[dz, p], sibling)

    def both(*conditions):
        joined = conditions[0]
        for condition in conditions[1:]:
            joined = jnp.logical_and(joined, condition)
        return joined

    def exists(dz):
        return z + dz < layers

    def goes(dz, at_start, at_end):
        if dz == lifted:
            return z == top
        if dz == 0:
            return at_start
        if fold and dz == depth:
            return both(exists(dz), at_end)
        return exists(dz)

    def z_tx(dz):
        if fold and dz + 1 == depth:
            return both(exists(dz), z >= 1, jnp.logical_or(z >= 2, q == 0))
        return both(exists(dz), z >= 1)

    def z_rx(dz):
        return goes(dz, None, q == 0)

    def c_tx(dz):
        return goes(dz, c == 1, q == 0)

    def c_rx(dz):
        return goes(dz, c == 0, q == 1)

    def y_tx(dz):
        return goes(dz, y == 1, q == 0)

    def y_rx(dz):
        return goes(dz, y == 0, q == 2)

    def detoured(dz, p):
        return fold and dz == depth - 1 and p == pieces - 1

    def over_tx(dz, p):
        if detoured(dz, p):
            return both(y_tx(dz), jnp.logical_or(z > 0, y == 0))
        if raised(dz, p):
            return both(y_tx(dz), y == 0)
        return y_tx(dz)

    def raised(dz, p):
        return fold and dz == lifted and p >= pieces // 2

    def lift_mate(p):
        return copy(held.at[mate_q, rows(p)], lifted * wide + mate_q, p,
                    e_send.at[lifted, p], y_recv.at[lifted, p], me + top * wide)

    def extra(dz, p):
        return copy(held.at[dz * wide + mate_q, rows(p)], (dz + 1) * wide + mate_q, p,
                    e_send.at[dz, p], y_recv.at[dz + 1, p], me - wide)

    def extra_tx():
        return both(z == 1, y == 0)

    def d_rx(dz):
        return goes(dz, y == 0, q == 3)

    def lift(p):
        return copy(white_ref.at[rows(p)], lifted * wide + q, p, z_send.at[lifted, p], z_recv.at[lifted, p],
                    me + top * wide)

    def sends(dz):
        for p in range(pieces):
            if dz > 0:
                @pl.when(z_rx(dz))
                def _():
                    from_above(dz, p).wait_recv()
            if dz < depth:
                @pl.when(z_tx(dz))
                def _():
                    down(dz, p).start()
            if columns == 2:
                @pl.when(over_tx(dz, p))
                def _():
                    over(dz, p, dz * wide + q).start()
            @pl.when(c_tx(dz))
            def _():
                across(dz, p, dz * wide + q).start()

    def passes(dz):
        if columns == 2:
            for p in range(pieces):
                @pl.when(y_rx(dz))
                def _():
                    over(dz, p, dz * wide + mate_q).wait_recv()
                    onward(dz, p, dz * wide + mate_q).start()
                if dz == 0 and raised(lifted, p):
                    @pl.when(both(z == 0, y == 0))
                    def _():
                        lift_mate(p).start()
                if detoured(dz + 1, p):
                    @pl.when(extra_tx())
                    def _():
                        extra(dz, p).start()

    def arrives(dz):
        for p in range(pieces):
            @pl.when(c_rx(dz))
            def _():
                across(dz, p, dz * wide + sib_q).wait_recv()
            if columns == 2:
                @pl.when(d_rx(dz))
                def _():
                    onward(dz, p, dz * wide + far_q).wait_recv()

    def finishes(dz):
        for p in range(pieces):
            if dz < depth:
                @pl.when(z_tx(dz))
                def _():
                    down(dz, p).wait_send()
            if columns == 2:
                @pl.when(over_tx(dz, p))
                def _():
                    over(dz, p, dz * wide + q).wait_send()
                if detoured(dz + 1, p):
                    @pl.when(extra_tx())
                    def _():
                        extra(dz, p).wait_send()
                @pl.when(y_rx(dz))
                def _():
                    onward(dz, p, dz * wide + mate_q).wait_send()
            @pl.when(c_tx(dz))
            def _():
                across(dz, p, dz * wide + q).wait_send()

    def answer(i):
        return pltpu.make_async_remote_copy(
            src_ref=made.at[i],
            dst_ref=back.at[q],
            send_sem=r_send.at[i],
            recv_sem=r_recv.at[q],
            device_id={"chan": jnp.int32(i)},
            device_id_type=pl.DeviceIdType.MESH,
        )

    def answered(i):
        return pltpu.make_async_remote_copy(
            src_ref=made.at[i],
            dst_ref=back.at[i],
            send_sem=r_send.at[i],
            recv_sem=r_recv.at[i],
            device_id={"chan": me},
            device_id_type=pl.DeviceIdType.MESH,
        )

    low = lax.broadcasted_iota(jnp.int32, (8, LANES), 0) < 4

    def prepare(i, carry):
        raw = white_ref[i]
        value = raw.astype(jnp.float32)
        own[i] = value
        ext[q * count + i] = raw
        for w in range(windows):
            swapped[i, w * 8 : w * 8 + 8] = pltpu.roll(value[w * 8 : w * 8 + 8], 4, 0)
        return carry

    def settle(dz):
        def one(l):
            def fill(i, carry):
                ext[(dz * wide + l) * count + i] = held[dz * wide + l, i]
                return carry
            lax.fori_loop(0, count, fill, 0, unroll=4)

        if dz == 0:
            for l in range(1, wide):
                @pl.when(q < l)
                def _():
                    one(l)
        else:
            @pl.when(exists(dz))
            def _():
                for l in range(1 if fold and dz == depth else wide):
                    one(l)

    live = jnp.minimum(layers * wide - me, pairs)

    def outside():
        def nothing(k, carry):
            for r in range(count):
                cross_ref[r, k] = jnp.zeros((8, LANES), jnp.float32)
            return carry

        lax.fori_loop(live, pairs, nothing, 0)

        @pl.when(layers - z <= depth)
        def _():
            def blank(i, carry):
                ext[(layers - z) * wide * count + i] = jnp.zeros((slab, LANES), jnp.bfloat16)
                return carry

            lax.fori_loop(0, 2 * count, blank, 0, unroll=4)

    def reached(dz):
        if dz < 0:
            return 0
        if dz == depth:
            return live
        return jnp.minimum((dz + 1) * wide - q - 1, live)

    def multiply(dz):
        def pair(k, carry):
            shift = offsets_ref[k]

            def channel(i, inner):
                place = me * count + i + shift
                keep = jnp.where(place < total, 1.0 / windows, 0.0)
                near = jnp.minimum(q * count + i + shift, ext.shape[0] - 1)
                partner = ext[near].astype(jnp.float32)
                straight = own[i, :8] * partner[:8]
                twisted = swapped[i, :8] * partner[:8]
                for w in range(1, windows):
                    part = slice(w * 8, w * 8 + 8)
                    straight += own[i, part] * partner[part]
                    twisted += swapped[i, part] * partner[part]
                joined = jnp.where(
                    low,
                    straight + pltpu.roll(straight, 4, 0),
                    pltpu.roll(twisted, 4, 0) - twisted,
                )
                cross_ref[i, k] = joined * keep
                return inner

            return lax.fori_loop(0, count, channel, carry, unroll=4)

        begin, end = reached(dz - 1), reached(dz)
        if fold and dz == depth:
            @pl.when(z == 0)
            def _():
                lax.fori_loop(begin, begin + 1, pair, 0)

            @pl.when(z > 0)
            def _():
                lax.fori_loop(begin, end, pair, 0)
        else:
            lax.fori_loop(begin, end, pair, 0)

    def reply():
        for i in range(wide):
            shift = offsets_ref[top * wide + q - i]

            def channel(r, carry):
                place = i * count + r + shift
                keep = jnp.where(place < total, 1.0 / windows, 0.0)
                near = jnp.clip(place - top * wide * count, 0, ext.shape[0] - 1)
                partner = ext[near].astype(jnp.float32)
                value = held[lifted * wide + i, r].astype(jnp.float32)
                straight = value[:8] * partner[:8]
                twisted = pltpu.roll(value[:8], 4, 0) * partner[:8]
                for w in range(1, windows):
                    part = slice(w * 8, w * 8 + 8)
                    straight += value[part] * partner[part]
                    twisted += pltpu.roll(value[part], 4, 0) * partner[part]
                joined = jnp.where(
                    low,
                    straight + pltpu.roll(straight, 4, 0),
                    pltpu.roll(twisted, 4, 0) - twisted,
                )
                made[i, r] = (joined * keep).astype(jnp.bfloat16)
                return carry

            lax.fori_loop(0, count, channel, 0, unroll=4)
        for i in range(wide):
            answer(i).start()

    sends(0)
    if fold:
        @pl.when(z == 0)
        def _():
            for p in range(pieces):
                lift(p).start()

    lax.fori_loop(0, count, prepare, 0)
    outside()
    for dz in range(depth + 1):
        if dz < depth:
            sends(dz + 1)
        if fold and dz == 0:
            sends(lifted)
        passes(dz)
        if fold and dz == 0:
            passes(lifted)
        arrives(dz)
        settle(dz)
        if fold and dz == 0:
            arrives(lifted)

            @pl.when(z == top)
            def _():
                reply()

        multiply(dz)

    if fold:
        @pl.when(z == 0)
        def _():
            for i in range(wide):
                answered(i).wait_recv()

                def take(r, carry):
                    cross_ref[r, top * wide - q + i] = back[i, r].astype(jnp.float32)
                    return carry

                lax.fori_loop(0, count, take, 0, unroll=4)
            for p in range(pieces):
                lift(p).wait_send()
                if raised(lifted, p):
                    @pl.when(y == 0)
                    def _():
                        lift_mate(p).wait_send()

        @pl.when(z == top)
        def _():
            for i in range(wide):
                answer(i).wait_send()

        finishes(lifted)
    for dz in range(depth + 1):
        finishes(dz)


def shards(columns, records, live_mask, offsets):
    count, windows, length = records.shape
    pairs = offsets.shape[0]
    wide = 2 * columns
    layers = lax.axis_size("chan") // wide
    reach = (BAND + count - 2) // count
    depth = min(layers - 1, (wide - 1 + reach) // wide)
    pieces = PIECES
    fold = columns == 2 and depth == layers - 1 and depth >= 2 and layers * wide == pairs and pairs * count == BAND
    spectra = whiten(records, live_mask).reshape(count, windows * 8, LANES)
    slots = (depth + 1) * wide
    cross = pl.pallas_call(
        functools.partial(reach_kernel, (layers, columns, depth, pieces, windows, fold)),
        out_shape=jax.ShapeDtypeStruct((count, pairs, 8, LANES), jnp.float32),
        in_specs=[
            pl.BlockSpec(memory_space=pltpu.SMEM),
            pl.BlockSpec(memory_space=pltpu.VMEM),
        ],
        out_specs=pl.BlockSpec(memory_space=pltpu.VMEM),
        scratch_shapes=[
            pltpu.VMEM((slots + wide, count, windows * 8, LANES), jnp.bfloat16),
            pltpu.VMEM((slots * count, windows * 8, LANES), jnp.bfloat16),
            pltpu.VMEM((count, windows * 8, LANES), jnp.float32),
            pltpu.VMEM((count, windows * 8, LANES), jnp.float32),
            pltpu.VMEM((wide, count, 8, LANES), jnp.bfloat16),
            pltpu.VMEM((wide, count, 8, LANES), jnp.bfloat16),
        ]
        + [pltpu.SemaphoreType.DMA((depth + 2, pieces))] * 9
        + [pltpu.SemaphoreType.DMA((wide,))] * 2,
        compiler_params=pltpu.CompilerParams(
            vmem_limit_bytes=40 * 1024 * 1024, collective_id=0, has_side_effects=True
        ),
    )(offsets, spectra)
    cross = cross.astype(jnp.bfloat16).reshape(count * pairs, 8 * LANES)
    result = jnp.dot(cross, jnp.asarray(inverse_table(length)), preferred_element_type=jnp.float32)
    result = result * (1.0 / math.sqrt(F))
    return result.reshape(count, pairs, LAGS).astype(jnp.bfloat16)


def solution(mesh):
    in_specs = (P(("day", "chan"), None, None), P(("day", "chan")), P())
    out_specs = P(("day", "chan"), None, None)
    columns = max(1, LAYER_CHIPS // mesh.shape["day"])
    body = functools.partial(shards, columns)
    return jax.shard_map(body, mesh=mesh, in_specs=in_specs, out_specs=out_specs, check_vma=False)
```

profile of v0, /device:TPU:0, one launch (start us, length us, event | category | flops | bytes accessed | tf_op | source)
XLA Modules:
  0.0 56.9 jit_solution(12340338501367269925)
XLA Ops:
  0.0 0.0 copy-start
  0.0 0.8 %convert_element_type.15 = f32[32]{0:T(128)S(1)} convert(s32[32]{0:T(128)} %param.6) | non-fusion elementwise | flops 32 | bytes 256 | tf_op jit(solution)/shard_map/convert_element_type | solution.py:45
  0.8 0.1 broadcast_in_dim.4
  0.9 0.1 broadcast_in_dim_reshape.3
  0.9 0.5 copy-done
  1.4 0.0 copy-start.1
  1.4 4.7 %multiply_reduce_fusion = (f32[256]{0:T(256)S(1)}, f32[1024,256]{1,0:T(8,128)S(1)}) fusion(bf16[3000,1024]{1,0:T(8,128)(2,1)} %constant.13.clone, bf16[32,8,3000]{2,1,0:T(8,128)(2,1)S(1)} %copy-done), kind=kOutput, calls=%fused_computation.6 | convolution fusion | flops 1573388032 | bytes 8729600 | tf_op jit(solution)/shard_map/dot_general | solution.py:39
  6.1 0.1 fusion.4
  6.2 0.2 copy.7
  6.5 0.2 reshape.27.white_ref
  6.7 0.0 copy-done.1
  6.7 0.0 copy-start.2
  6.7 46.3 %shard_map.55 = f32[32,16,8,128]{3,2,1,0:T(8,128)S(1)} custom-call(s32[16]{0:T(128)S(1)} %copy-done.1, bf16[32,64,128]{2,1,0:T(8,128)(2,1)S(1)} %reshape.27.white_ref), custom_call_target="tpu_custom_call" | custom-call | tf_op jit(solution)/shard_map/pallas_call | solution.py:472
  53.1 0.2 convert_element_type.17
  53.2 0.0 copy-done.2
  53.2 3.7 %multiply_convert_fusion = bf16[512,2048]{1,0:T(8,128)(2,1)} fusion(bf16[1024,2048]{1,0:T(8,128)(2,1)S(1)} %copy-done.2, bf16[64,8,8,128]{3,2,1,0:T(8,128)(2,1)S(1)} %bitcast.15), kind=kOutput, calls=%fused_computation | convolution fusion | flops 2149580800 | bytes 7340032 | tf_op jit(solution)/shard_map/dot_general | solution.py:495
  (1 shorter events, 0.0 us)
Async XLA Ops:
  0.0 1.4 %copy-start = (bf16[32,8,3000]{2,1,0:T(8,128)(2,1)S(1)}, bf16[32,8,3000]{2,1,0:T(8,128)(2,1)}, u32[]{:S(2)}) copy-start(bf16[32,8,3000]{2,1,0:T(8,128)(2,1)} %param.5) | copy-start | bytes 4608004
  1.4 5.3 %copy-start.1 = (s32[16]{0:T(128)S(1)}, s32[16]{0:T(128)}, u32[]{:S(2)}) copy-start(s32[16]{0:T(128)} %offsets_ref.1) | copy-start | bytes 196
  6.7 46.5 %copy-start.2 = (bf16[1024,2048]{1,0:T(8,128)(2,1)S(1)}, bf16[1024,2048]{1,0:T(8,128)(2,1)}, u32[]{:S(2)}) copy-start(bf16[1024,2048]{1,0:T(8,128)(2,1)} %constant.14.clone) | copy-start | bytes 12582916
where the time goes:
time: 57.6 us; the launch traced here: 56.9 us
  Pallas kernels  46.3 us (80%)
  matrix products  8.35 us (14%)
  local copies, waits for them, and re-layouts  1.09 us (2%)
  other arithmetic  1.05 us (2%)
    pallas_call x1, Pallas kernels, shards(): pl.pallas_call(functools.partial(reach_kernel, (layers, columns, depth, p...  46.3 us
    dot_general x1, matrix products, whiten(): jnp.dot(records.reshape(count * windows, length), jnp.asarray(forward_tab...  4.69 us
    dot_general x1, matrix products, shards(): jnp.dot(cross, jnp.asarray(inverse_table(length)), preferred_element_type...  3.66 us

commit v1 on v0

--- a/solution.py
+++ b/solution.py
@@ -458,6 +458,301 @@
         finishes(dz)
 
 
+def middle_kernel(shape, offsets_ref, white_ref, cross_ref, held, spec, made, back, joined,
+                  x_send, f_send, s_recv, r_send, r_recv):
+    layers, wide, windows = shape
+    pairs = offsets_ref.shape[0]
+    count = white_ref.shape[0] // windows
+    parts = layers * wide
+    pitch = spec.shape[0] // (2 * windows)
+    half, top, last = layers // 2, layers - 1, parts - 1
+    me = lax.axis_index("chan")
+    z, q = me // wide, me % wide
+    c = q % 2
+    first = z * wide
+    base = half * wide
+    sib_q = q + 1 - 2 * c
+    mate_q = (q + 2) % wide
+    far_q = (sib_q + 2) % wide
+    inner_low, inner_high = z == half - 1, z == half
+    meets = jnp.logical_or(
+        jnp.logical_and(inner_low, c == 0), jnp.logical_and(inner_high, c == 1))
+    ships = jnp.logical_not(meets)
+    neighbour = jnp.where(z < half, me + wide, me - wide)
+
+    barrier = pltpu.get_barrier_semaphore()
+    for i in range(parts):
+        @pl.when(me != i)
+        def _():
+            pl.semaphore_signal(barrier, inc=1, device_id={"chan": jnp.int32(i)},
+                                device_id_type=pl.DeviceIdType.MESH)
+    pl.semaphore_wait(barrier, parts - 1)
+
+    def remote(source, target, send, recv, device):
+        return pltpu.make_async_remote_copy(
+            src_ref=source, dst_ref=target, send_sem=send, recv_sem=recv,
+            device_id={"chan": device}, device_id_type=pl.DeviceIdType.MESH,
+        )
+
+    def piece(ri, col):
+        return white_ref.at[:, pl.ds(pl.multiple_of((ri * wide + col) * LANES, LANES), LANES)]
+
+    def swap(j, ri, col):
+        return remote(piece(ri, col), held.at[me, ri], x_send.at[j, ri], s_recv.at[me, ri], first + col)
+
+    def ship_own(ri):
+        return remote(piece(ri, q), held.at[me, ri], f_send.at[me, ri], s_recv.at[me, ri], neighbour)
+
+    def ship(s, ri):
+        return remote(held.at[s, ri], held.at[s, ri], f_send.at[s, ri], s_recv.at[s, ri], neighbour)
+
+    def reply(d, k):
+        return remote(made.at[d, k], back.at[k, q], r_send.at[d, k], r_recv.at[k, q], d)
+
+    def replied(k, col):
+        return remote(back.at[k, col], back.at[k, col], r_send.at[me, k], r_recv.at[k, col], me)
+
+    behind = jnp.logical_and(z == top, q >= 2)
+    ahead = jnp.logical_and(ships, jnp.logical_not(behind))
+
+    @pl.when(ahead)
+    def _():
+        for ri in range(2):
+            ship_own(ri).start()
+    columns = (sib_q, mate_q, far_q)
+    for j, col in enumerate(columns):
+        for ri in range(2):
+            swap(j, ri, col).start()
+
+    def settle(s, load):
+        for ri in range(2):
+            def one(i, carry):
+                value = load(ri, i).astype(jnp.float32)
+                for part in range(2):
+                    row = ri * windows * pitch + s * count + 2 * i + part
+                    spec[pl.ds(row, windows, stride=pitch), :] = value[part * windows:(part + 1) * windows]
+                return carry
+
+            lax.fori_loop(0, count // 2, one, 0, unroll=4)
+
+    def own_rows(ri, i):
+        lanes = pl.ds(pl.multiple_of((ri * wide + q) * LANES, LANES), LANES)
+        return white_ref[pl.ds(pl.multiple_of(i * 2 * windows, 2 * windows), 2 * windows), lanes]
+
+    def take(s, onward):
+        for ri in range(2):
+            ship(s, ri).wait_recv()
+
+        if onward is not False:
+            @pl.when(onward)
+            def _():
+                for ri in range(2):
+                    ship(s, ri).start()
+        settle(s, lambda ri, i: held[s, ri, pl.ds(pl.multiple_of(i * 2 * windows, 2 * windows), 2 * windows)])
+
+    def block(d, k):
+        shift = offsets_ref[k]
+        for g in range(count // 16):
+            mine = d * count + g * 16
+            real = imag = None
+            for w in range(windows):
+                cr = spec[pl.ds(pl.multiple_of(w * pitch + mine, 8), 16), :]
+                ci = spec[pl.ds(pl.multiple_of((windows + w) * pitch + mine, 8), 16), :]
+                pr = spec[pl.ds(w * pitch + mine + shift, 16), :]
+                pi = spec[pl.ds((windows + w) * pitch + mine + shift, 16), :]
+                re, im = cr * pr + ci * pi, ci * pr - cr * pi
+                real, imag = (re, im) if w == 0 else (real + re, imag + im)
+            rows = slice(g * 16, g * 16 + 16)
+            made[d, k, 0, rows] = (real * (1.0 / windows)).astype(jnp.bfloat16)
+            made[d, k, 1, rows] = (imag * (1.0 / windows)).astype(jnp.bfloat16)
+
+    def blocks(d_begin, d_end, u_begin, u_end):
+        def reach(u, carry):
+            low, high = jnp.maximum(d_begin, u - pairs), jnp.minimum(d_end, u)
+
+            def work(d, inner):
+                block(d, u - 1 - d)
+                return inner
+
+            def give(d, inner):
+                @pl.when(d != me)
+                def _():
+                    reply(d, u - 1 - d).start()
+                return inner
+
+            lax.fori_loop(low, high, work, 0)
+            lax.fori_loop(low, high, give, 0)
+            return carry
+
+        lax.fori_loop(u_begin, u_end, reach, 0)
+
+    for x in range(2 * windows):
+        spec[pl.ds(x * pitch + parts * count, count), :] = jnp.zeros((count, LANES), jnp.float32)
+
+    def clear(i, carry):
+        joined[pl.ds(pl.multiple_of(i * 64, 64), 64), :] = jnp.zeros((64, LANES), jnp.float32)
+        return carry
+
+    lax.fori_loop(0, joined.shape[0] // 64, clear, 0)
+
+    settle(me, own_rows)
+    take(first + sib_q, ahead)
+    take(first + mate_q, ships)
+    take(first + far_q, ships)
+
+    @pl.when(behind)
+    def _():
+        for ri in range(2):
+            ship_own(ri).start()
+            ship(first + sib_q, ri).start()
+
+    def nearest(j):
+        return jnp.where(j == 0, q, jnp.where(j == 1, sib_q, jnp.where(j == 2, mate_q, far_q)))
+
+    blocks(first, first + wide, first + 1, first + wide + jnp.where(z == top, 1, 0))
+
+    @pl.when(jnp.logical_and(inner_low, c == 0))
+    def _():
+        def step(s, carry):
+            take(s, False)
+            blocks(first, first + wide, s, s + 1)
+            return carry
+        lax.fori_loop(base, base + wide, step, 0)
+
+    @pl.when(jnp.logical_and(inner_high, c == 1))
+    def _():
+        def step(j, carry):
+            s = base - wide + nearest(j)
+            take(s, False)
+            blocks(s, s + 1, base + 1, base + wide)
+            return carry
+        lax.fori_loop(0, wide, step, 0)
+        blocks(base - wide, base, base, base + 1)
+
+    @pl.when(jnp.logical_or(inner_low, jnp.logical_and(inner_high, c == 1)))
+    def _():
+        begin = jnp.where(inner_low, first + 1, first)
+        end = jnp.where(jnp.logical_and(inner_low, c == 0), base + wide, first + wide)
+
+        def step(j, carry):
+            s = nearest(j)
+            take(s, ships)
+            blocks(s, s + 1, begin, end)
+            return carry
+        lax.fori_loop(0, wide, step, 0)
+        blocks(0, wide, first, begin)
+
+    @pl.when(jnp.logical_or(inner_high, jnp.logical_and(inner_low, c == 0)))
+    def _():
+        begin = jnp.where(jnp.logical_and(inner_high, c == 0), first, 0)
+
+        def step(s, carry):
+            take(s, ships)
+            blocks(begin, first + wide, s, s + 1 + jnp.where(s == last, 1, 0))
+            return carry
+        lax.fori_loop(top * wide, parts, step, 0)
+
+    def unpack(source, k, col):
+        for ri in range(2):
+            for g in range(count // 16):
+                value = source[ri, g * 16:g * 16 + 16].astype(jnp.float32)
+                for part in range(2):
+                    row = (ri * wide + col) * count * pairs + (g * 16 + part * 8) * pairs + k
+                    joined[pl.ds(row, 8, stride=pairs), :] = value[part * 8:part * 8 + 8]
+
+    def collect(k, carry):
+        u = me + k + 1
+        away = jnp.logical_or(
+            jnp.logical_and(z == 0, u >= wide),
+            jnp.logical_and(jnp.logical_and(inner_low, c == 1), u >= base))
+        for col in range(wide):
+            here = jnp.logical_and(q == col, jnp.logical_not(away))
+
+            @pl.when(here)
+            def _():
+                unpack(made.at[me, k], k, col)
+
+            @pl.when(jnp.logical_not(here))
+            def _():
+                replied(k, col).wait_recv()
+                unpack(back.at[k, col], k, col)
+        return carry
+
+    lax.fori_loop(0, parts - me, collect, 0)
+
+    def pack(i, carry):
+        rows = pl.ds(pl.multiple_of(i * 16, 16), 16)
+        for x in range(2 * wide):
+            start = pl.multiple_of(x * count * pairs + i * 16, 16)
+            cross_ref[rows, x * LANES:(x + 1) * LANES] = joined[pl.ds(start, 16), :].astype(jnp.bfloat16)
+        return carry
+
+    lax.fori_loop(0, count * pairs // 16, pack, 0, unroll=2)
+
+    for j, col in enumerate(columns):
+        for ri in range(2):
+            swap(j, ri, col).wait_send()
+
+    @pl.when(ships)
+    def _():
+        def sent(s, carry):
+            for ri in range(2):
+                ship(s, ri).wait_send()
+            return carry
+
+        lax.fori_loop(first, first + wide, sent, 0)
+
+        @pl.when(jnp.logical_or(inner_low, inner_high))
+        def _():
+            begin = jnp.where(inner_low, 0, top * wide)
+            lax.fori_loop(begin, begin + wide, sent, 0)
+
+    d_begin = jnp.where(jnp.logical_or(z == top, jnp.logical_and(inner_high, c == 0)), first, 0)
+    u_end = jnp.where(jnp.logical_or(z == 0, jnp.logical_and(inner_low, c == 1)), first + wide, parts + 1)
+
+    def drained(u, carry):
+        def one(d, inner):
+            @pl.when(d != me)
+            def _():
+                reply(d, u - 1 - d).wait_send()
+            return inner
+
+        return lax.fori_loop(jnp.maximum(d_begin, u - pairs), jnp.minimum(first + wide, u), one, carry)
+
+    lax.fori_loop(jnp.maximum(first, 1), u_end, drained, 0)
+
+
+def meet(layers, wide, white, windows, offsets):
+    pairs = offsets.shape[0]
+    count = white.shape[0] // windows
+    parts = layers * wide
+    pitch = (parts + 1) * count
+    return pl.pallas_call(
+        functools.partial(middle_kernel, (layers, wide, windows)),
+        out_shape=jax.ShapeDtypeStruct((count * pairs, 2 * F), jnp.bfloat16),
+        in_specs=[
+            pl.BlockSpec(memory_space=pltpu.SMEM),
+            pl.BlockSpec(memory_space=pltpu.VMEM),
+        ],
+        out_specs=pl.BlockSpec(memory_space=pltpu.VMEM),
+        scratch_shapes=[
+            pltpu.VMEM((parts, 2, count * windows, LANES), jnp.bfloat16),
+            pltpu.VMEM((2 * windows * pitch, LANES), jnp.float32),
+            pltpu.VMEM((parts, pairs, 2, count, LANES), jnp.bfloat16),
+            pltpu.VMEM((pairs, wide, 2, count, LANES), jnp.bfloat16),
+            pltpu.VMEM((2 * wide * count * pairs, LANES), jnp.float32),
+            pltpu.SemaphoreType.DMA((wide - 1, 2)),
+            pltpu.SemaphoreType.DMA((parts, 2)),
+            pltpu.SemaphoreType.DMA((parts, 2)),
+            pltpu.SemaphoreType.DMA((parts, pairs)),
+            pltpu.SemaphoreType.DMA((pairs, wide)),
+        ],
+        compiler_params=pltpu.CompilerParams(
+            vmem_limit_bytes=40 * 1024 * 1024, collective_id=1, has_side_effects=True
+        ),
+    )(offsets, white)
+
+
 def shards(columns, records, live_mask, offsets):
     count, windows, length = records.shape
     pairs = offsets.shape[0]
@@ -467,7 +762,14 @@
     depth = min(layers - 1, (wide - 1 + reach) // wide)
     pieces = PIECES
     fold = columns == 2 and depth == layers - 1 and depth >= 2 and layers * wide == pairs and pairs * count == BAND
-    spectra = whiten(records, live_mask).reshape(count, windows * 8, LANES)
+    white = whiten(records, live_mask)
+    if (
+        columns == 2 and layers == 4 and layers * wide == pairs and pairs * count == BAND
+        and F == wide * LANES and windows == 8 and count % 16 == 0
+    ):
+        cross = meet(layers, wide, white, windows, offsets)
+        return lags(cross, count, pairs, length)
+    spectra = white.reshape(count, windows * 8, LANES)
     slots = (depth + 1) * wide
     cross = pl.pallas_call(
         functools.partial(reach_kernel, (layers, columns, depth, pieces, windows, fold)),
@@ -491,7 +793,10 @@
             vmem_limit_bytes=40 * 1024 * 1024, collective_id=0, has_side_effects=True
         ),
     )(offsets, spectra)
-    cross = cross.astype(jnp.bfloat16).reshape(count * pairs, 8 * LANES)
+    return lags(cross.astype(jnp.bfloat16).reshape(count * pairs, 8 * LANES), count, pairs, length)
+
+
+def lags(cross, count, pairs, length):
     result = jnp.dot(cross, jnp.asarray(inverse_table(length)), preferred_element_type=jnp.float32)
     result = result * (1.0 / math.sqrt(F))
     return result.reshape(count, pairs, LAGS).astype(jnp.bfloat16)

time: 57.6 us -> 56.3 us (0.977)
  Pallas kernels: 46.3 us -> 41.4 us
  matrix products: 8.35 us -> 11.5 us
  local copies, waits for them, and re-layouts: 1.09 us -> 2.21 us
    pallas_call x1, Pallas kernels: 46.3 us -> 41.4 us  [meet(): pl.pallas_call(functools.partial(middle_kernel, (layers, wide, windows)),...]
    dot_general x1, matrix products: 3.66 us -> 5.85 us  [lags(): jnp.dot(cross, jnp.asarray(inverse_table(length)), preferred_element_type...]
    dot_general x0 -> x1, local copies, waits for them, and re-layouts: none -> 1.56 us  [whiten(): jnp.dot(records.reshape(count * windows, length), jnp.asarray(forward_tab...]
    dot_general x1, matrix products: 4.69 us -> 5.65 us  [whiten(): jnp.dot(records.reshape(count * windows, length), jnp.asarray(forward_tab...]
where the time goes in v1:
time: 56.3 us; the launch traced here: 56.1 us
  Pallas kernels  41.4 us (74%)
  matrix products  11.5 us (20%)
  local copies, waits for them, and re-layouts  2.21 us (4%)
  other arithmetic  0.91 us (2%)
    pallas_call x1, Pallas kernels, meet(): pl.pallas_call(functools.partial(middle_kernel, (layers, wide, windows)),...  41.4 us
    dot_general x1, matrix products, lags(): jnp.dot(cross, jnp.asarray(inverse_table(length)), preferred_element_type...  5.85 us
    dot_general x1, matrix products, whiten(): jnp.dot(records.reshape(count * windows, length), jnp.asarray(forward_tab...  5.65 us
    dot_general x1, local copies, waits for them, and re-layouts, whiten(): jnp.dot(records.reshape(count * windows, length), jnp.asarray(forward_tab...  1.56 us

profile of v1, /device:TPU:0, one launch (start us, length us, event | category | flops | bytes accessed | tf_op | source)
XLA Modules:
  0.0 56.1 jit_solution(7852636418402297450)
XLA Ops:
  0.0 0.0 copy-start
  0.0 0.8 %convert_element_type.12 = f32[32]{0:T(128)S(1)} convert(s32[32]{0:T(128)} %param.6) | non-fusion elementwise | flops 32 | bytes 256 | tf_op jit(solution)/shard_map/convert_element_type | solution.py:45
  0.8 0.1 broadcast_in_dim.4
  0.9 0.1 broadcast_in_dim_reshape.3
  0.9 0.5 copy-done
  1.4 0.0 copy-start.1
  1.4 5.7 %multiply_reduce_fusion = (f32[256]{0:T(256)S(1)}, f32[1024,256]{1,0:T(8,128)}) fusion(bf16[3000,1024]{1,0:T(8,128)(2,1)} %constant.13.clone, bf16[32,8,3000]{2,1,0:T(8,128)(2,1)S(1)} %copy-done), kind=kOutput, calls=%fused_computation.4 | convolution fusion | flops 1573388032 | bytes 8729600 | tf_op jit(solution)/shard_map/dot_general | solution.py:39
  7.1 1.6 %copy.7 = f32[1024,256]{0,1:T(8,128)S(1)} copy(f32[1024,256]{1,0:T(8,128)} %get-tuple-element.6) | data formatting | bytes 2097152 | tf_op jit(solution)/shard_map/dot_general | solution.py:39
  8.7 0.1 fusion.2.white_ref
  8.8 0.0 copy-done.1
  8.8 41.4 %shard_map.55 = bf16[512,1024]{1,0:T(8,128)(2,1)S(1)} custom-call(s32[16]{0:T(128)S(1)} %copy-done.1, bf16[256,1024]{1,0:T(8,128)(2,1)S(1)} %fusion.2.white_ref), custom_call_target="tpu_custom_call" | custom-call | tf_op jit(solution)/shard_map/pallas_call | solution.py:730
  50.3 5.9 %multiply_convert_fusion = bf16[512,2048]{1,0:T(8,128)(2,1)} fusion(bf16[512,1024]{1,0:T(8,128)(2,1)S(1)} %shard_map.55, bf16[1024,2048]{1,0:T(8,128)(2,1)} %constant.14.clone), kind=kOutput, calls=%fused_computation | convolution fusion | flops 2149580800 | bytes 7340032 | tf_op jit(solution)/shard_map/dot_general | solution.py:800
  (1 shorter events, 0.0 us)
Async XLA Ops:
  0.0 1.4 %copy-start = (bf16[32,8,3000]{2,1,0:T(8,128)(2,1)S(1)}, bf16[32,8,3000]{2,1,0:T(8,128)(2,1)}, u32[]{:S(2)}) copy-start(bf16[32,8,3000]{2,1,0:T(8,128)(2,1)} %param.5) | copy-start | bytes 4608004
  1.4 7.4 %copy-start.1 = (s32[16]{0:T(128)S(1)}, s32[16]{0:T(128)}, u32[]{:S(2)}) copy-start(s32[16]{0:T(128)} %offsets_ref.1) | copy-start | bytes 196

commit v2 on v1

--- a/solution.py
+++ b/solution.py
@@ -474,19 +474,41 @@
     sib_q = q + 1 - 2 * c
     mate_q = (q + 2) % wide
     far_q = (sib_q + 2) % wide
+    near = c == 0
     inner_low, inner_high = z == half - 1, z == half
-    meets = jnp.logical_or(
-        jnp.logical_and(inner_low, c == 0), jnp.logical_and(inner_high, c == 1))
-    ships = jnp.logical_not(meets)
-    neighbour = jnp.where(z < half, me + wide, me - wide)
+    neighbour = jnp.where(
+        jnp.logical_or(z == 0, jnp.logical_and(inner_low, c == 1)), me + wide, me - wide)
+    own_end = jnp.where(
+        z == 0, jnp.where(near, base, wide),
+        jnp.where(jnp.logical_and(inner_low, c == 1), base + wide, parts + 1))
+    low_begin = jnp.where(
+        inner_low, jnp.where(near, base, wide),
+        jnp.where(jnp.logical_and(inner_high, c == 1), base + wide, 0))
+    low_end = jnp.where(
+        inner_low, own_end, jnp.where(jnp.logical_and(inner_high, c == 1), parts + 1, 0))
 
     barrier = pltpu.get_barrier_semaphore()
-    for i in range(parts):
-        @pl.when(me != i)
-        def _():
-            pl.semaphore_signal(barrier, inc=1, device_id={"chan": jnp.int32(i)},
+
+    def greet(device, condition):
+        @pl.when(condition)
+        def _():
+            pl.semaphore_signal(barrier, inc=1, device_id={"chan": jnp.int32(device)},
                                 device_id_type=pl.DeviceIdType.MESH)
-    pl.semaphore_wait(barrier, parts - 1)
+
+    for col in (sib_q, mate_q, far_q):
+        greet(first + col, z >= 0)
+    for i in range(wide):
+        odd = i % 2 == 1
+        greet(wide + i, z == 0)
+        if odd:
+            greet(base + i, z < half)
+        else:
+            greet(base + i, jnp.logical_and(inner_low, q == i))
+    greet(me - wide, jnp.logical_or(inner_low, jnp.logical_and(inner_high, c == 1)))
+    greet(me + wide, inner_high)
+    replies_far = jnp.where(inner_low, wide, jnp.where(jnp.logical_and(inner_high, c == 1), 2 * wide - 1, 0))
+    ships_there = jnp.where(jnp.logical_and(inner_low, near), 0, 1)
+    pl.semaphore_wait(barrier, wide - 1 + replies_far + ships_there)
 
     def remote(source, target, send, recv, device):
         return pltpu.make_async_remote_copy(
@@ -512,13 +534,8 @@
     def replied(k, col):
         return remote(back.at[k, col], back.at[k, col], r_send.at[me, k], r_recv.at[k, col], me)
 
-    behind = jnp.logical_and(z == top, q >= 2)
-    ahead = jnp.logical_and(ships, jnp.logical_not(behind))
-
-    @pl.when(ahead)
-    def _():
-        for ri in range(2):
-            ship_own(ri).start()
+    for ri in range(2):
+        ship_own(ri).start()
     columns = (sib_q, mate_q, far_q)
     for j, col in enumerate(columns):
         for ri in range(2):
@@ -539,11 +556,10 @@
         lanes = pl.ds(pl.multiple_of((ri * wide + q) * LANES, LANES), LANES)
         return white_ref[pl.ds(pl.multiple_of(i * 2 * windows, 2 * windows), 2 * windows), lanes]
 
-    def take(s, onward):
+    def take(s, onward=None):
         for ri in range(2):
             ship(s, ri).wait_recv()
-
-        if onward is not False:
+        if onward is not None:
             @pl.when(onward)
             def _():
                 for ri in range(2):
@@ -566,25 +582,29 @@
             made[d, k, 0, rows] = (real * (1.0 / windows)).astype(jnp.bfloat16)
             made[d, k, 1, rows] = (imag * (1.0 / windows)).astype(jnp.bfloat16)
 
-    def blocks(d_begin, d_end, u_begin, u_end):
+    def spans(d_begin, d_end, u_begin, u_end, visit):
         def reach(u, carry):
-            low, high = jnp.maximum(d_begin, u - pairs), jnp.minimum(d_end, u)
-
-            def work(d, inner):
-                block(d, u - 1 - d)
+            def one(d, inner):
+                visit(d, u - 1 - d)
                 return inner
 
-            def give(d, inner):
-                @pl.when(d != me)
-                def _():
-                    reply(d, u - 1 - d).start()
-                return inner
-
-            lax.fori_loop(low, high, work, 0)
-            lax.fori_loop(low, high, give, 0)
-            return carry
+            return lax.fori_loop(jnp.maximum(d_begin, u - pairs), jnp.minimum(d_end, u), one, carry)
 
         lax.fori_loop(u_begin, u_end, reach, 0)
+
+    def give(d, k):
+        @pl.when(d != me)
+        def _():
+            reply(d, k).start()
+
+    def gave(d, k):
+        @pl.when(d != me)
+        def _():
+            reply(d, k).wait_send()
+
+    def blocks(*span):
+        spans(*span, block)
+        spans(*span, give)
 
     for x in range(2 * windows):
         spec[pl.ds(x * pitch + parts * count, count), :] = jnp.zeros((count, LANES), jnp.float32)
@@ -595,62 +615,68 @@
 
     lax.fori_loop(0, joined.shape[0] // 64, clear, 0)
 
+    y = q // 2
+    pair_1, pair_2 = (q, sib_q), (mate_q, far_q)
+
+    def reached_1(start, more=0):
+        return jnp.where(y == 0, start, start + 3), jnp.where(y == 0, start + 2, start + wide + more)
+
+    def reached_2(start, more=0):
+        return jnp.where(y == 0, start + 2, start), jnp.where(y == 0, start + wide + more, start + 3)
+
     settle(me, own_rows)
-    take(first + sib_q, ahead)
-    take(first + mate_q, ships)
-    take(first + far_q, ships)
-
-    @pl.when(behind)
+    for col in columns:
+        take(first + col, z >= 0)
+    blocks(first, first + wide, first + 1, first + wide + jnp.where(z == top, 1, 0))
+
+    @pl.when(jnp.logical_and(z == 0, near))
     def _():
-        for ri in range(2):
-            ship_own(ri).start()
-            ship(first + sib_q, ri).start()
-
-    def nearest(j):
-        return jnp.where(j == 0, q, jnp.where(j == 1, sib_q, jnp.where(j == 2, mate_q, far_q)))
-
-    blocks(first, first + wide, first + 1, first + wide + jnp.where(z == top, 1, 0))
-
-    @pl.when(jnp.logical_and(inner_low, c == 0))
+        for group, reached in ((pair_1, reached_1), (pair_2, reached_2)):
+            for col in group:
+                take(wide + col)
+            blocks(0, wide, *reached(wide))
+
+    @pl.when(inner_low)
     def _():
-        def step(s, carry):
-            take(s, False)
-            blocks(first, first + wide, s, s + 1)
-            return carry
-        lax.fori_loop(base, base + wide, step, 0)
-
-    @pl.when(jnp.logical_and(inner_high, c == 1))
+        def lower(group):
+            for col in group:
+                take(col, jnp.logical_not(near))
+
+        lower(pair_1)
+        for col in pair_1:
+            take(base + col)
+        blocks(wide, base, *reached_1(base))
+        lower(pair_2)
+        blocks(0, wide, *reached_1(base))
+
+        @pl.when(jnp.logical_not(near))
+        def _():
+            blocks(0, wide, wide, base)
+        for col in pair_2:
+            take(base + col)
+        blocks(0, base, *reached_2(base))
+
+        @pl.when(near)
+        def _():
+            for group, reached in ((pair_1, reached_1), (pair_2, reached_2)):
+                for col in group:
+                    take(top * wide + col)
+                blocks(0, base, *reached(top * wide, 1))
+
+    @pl.when(inner_high)
     def _():
-        def step(j, carry):
-            s = base - wide + nearest(j)
-            take(s, False)
-            blocks(s, s + 1, base + 1, base + wide)
-            return carry
-        lax.fori_loop(0, wide, step, 0)
-        blocks(base - wide, base, base, base + 1)
-
-    @pl.when(jnp.logical_or(inner_low, jnp.logical_and(inner_high, c == 1)))
-    def _():
-        begin = jnp.where(inner_low, first + 1, first)
-        end = jnp.where(jnp.logical_and(inner_low, c == 0), base + wide, first + wide)
-
-        def step(j, carry):
-            s = nearest(j)
-            take(s, ships)
-            blocks(s, s + 1, begin, end)
-            return carry
-        lax.fori_loop(0, wide, step, 0)
-        blocks(0, wide, first, begin)
-
-    @pl.when(jnp.logical_or(inner_high, jnp.logical_and(inner_low, c == 0)))
-    def _():
-        begin = jnp.where(jnp.logical_and(inner_high, c == 0), first, 0)
-
-        def step(s, carry):
-            take(s, ships)
-            blocks(begin, first + wide, s, s + 1 + jnp.where(s == last, 1, 0))
-            return carry
-        lax.fori_loop(top * wide, parts, step, 0)
+        for group, reached in ((pair_1, reached_1), (pair_2, reached_2)):
+            for col in group:
+                take(top * wide + col, near)
+            blocks(base, base + wide, *reached(top * wide, 1))
+
+        @pl.when(jnp.logical_not(near))
+        def _():
+            for col in pair_1 + pair_2:
+                take(wide + col)
+            for col in pair_1 + pair_2:
+                take(col)
+            blocks(0, base, top * wide, parts + 1)
 
     def unpack(source, k, col):
         for ri in range(2):
@@ -661,10 +687,7 @@
                     joined[pl.ds(row, 8, stride=pairs), :] = value[part * 8:part * 8 + 8]
 
     def collect(k, carry):
-        u = me + k + 1
-        away = jnp.logical_or(
-            jnp.logical_and(z == 0, u >= wide),
-            jnp.logical_and(jnp.logical_and(inner_low, c == 1), u >= base))
+        away = me + k + 1 >= own_end
         for col in range(wide):
             here = jnp.logical_and(q == col, jnp.logical_not(away))
 
@@ -693,33 +716,20 @@
         for ri in range(2):
             swap(j, ri, col).wait_send()
 
-    @pl.when(ships)
+    def sent(s, carry):
+        for ri in range(2):
+            ship(s, ri).wait_send()
+        return carry
+
+    lax.fori_loop(first, first + wide, sent, 0)
+
+    @pl.when(jnp.logical_or(jnp.logical_and(inner_low, c == 1), jnp.logical_and(inner_high, near)))
     def _():
-        def sent(s, carry):
-            for ri in range(2):
-                ship(s, ri).wait_send()
-            return carry
-
-        lax.fori_loop(first, first + wide, sent, 0)
-
-        @pl.when(jnp.logical_or(inner_low, inner_high))
-        def _():
-            begin = jnp.where(inner_low, 0, top * wide)
-            lax.fori_loop(begin, begin + wide, sent, 0)
-
-    d_begin = jnp.where(jnp.logical_or(z == top, jnp.logical_and(inner_high, c == 0)), first, 0)
-    u_end = jnp.where(jnp.logical_or(z == 0, jnp.logical_and(inner_low, c == 1)), first + wide, parts + 1)
-
-    def drained(u, carry):
-        def one(d, inner):
-            @pl.when(d != me)
-            def _():
-                reply(d, u - 1 - d).wait_send()
-            return inner
-
-        return lax.fori_loop(jnp.maximum(d_begin, u - pairs), jnp.minimum(first + wide, u), one, carry)
-
-    lax.fori_loop(jnp.maximum(first, 1), u_end, drained, 0)
+        begin = jnp.where(inner_low, 0, top * wide)
+        lax.fori_loop(begin, begin + wide, sent, 0)
+
+    spans(first, first + wide, first + 1, own_end, gave)
+    spans(0, first, low_begin, low_end, gave)
 
 
 def meet(layers, wide, white, windows, offsets):

time: 56.3 us -> 53.1 us (0.943)
  Pallas kernels: 41.4 us -> 38.2 us
    pallas_call x1, Pallas kernels: 41.4 us -> 38.2 us  [meet(): pl.pallas_call(functools.partial(middle_kernel, (layers, wide, windows)),...]
where the time goes in v2:
time: 53.1 us; the launch traced here: 52.9 us
  Pallas kernels  38.2 us (72%)
  matrix products  11.5 us (22%)
  local copies, waits for them, and re-layouts  2.21 us (4%)
  other arithmetic  0.91 us (2%)
    pallas_call x1, Pallas kernels, meet(): pl.pallas_call(functools.partial(middle_kernel, (layers, wide, windows)),...  38.2 us
    dot_general x1, matrix products, lags(): jnp.dot(cross, jnp.asarray(inverse_table(length)), preferred_element_type...  5.85 us
    dot_general x1, matrix products, whiten(): jnp.dot(records.reshape(count * windows, length), jnp.asarray(forward_tab...  5.65 us
    dot_general x1, local copies, waits for them, and re-layouts, whiten(): jnp.dot(records.reshape(count * windows, length), jnp.asarray(forward_tab...  1.56 us

profile of v2, /device:TPU:0, one launch (start us, length us, event | category | flops | bytes accessed | tf_op | source)
XLA Modules:
  0.0 52.9 jit_solution(15477646164420553791)
XLA Ops:
  0.0 0.0 copy-start
  0.0 0.8 %convert_element_type.12 = f32[32]{0:T(128)S(1)} convert(s32[32]{0:T(128)} %param.6) | non-fusion elementwise | flops 32 | bytes 256 | tf_op jit(solution)/shard_map/convert_element_type | solution.py:45
  0.8 0.1 broadcast_in_dim.4
  0.9 0.1 broadcast_in_dim_reshape.3
  0.9 0.5 copy-done
  1.4 0.0 copy-start.1
  1.4 5.7 %multiply_reduce_fusion = (f32[256]{0:T(256)S(1)}, f32[1024,256]{1,0:T(8,128)}) fusion(bf16[3000,1024]{1,0:T(8,128)(2,1)} %constant.13.clone, bf16[32,8,3000]{2,1,0:T(8,128)(2,1)S(1)} %copy-done), kind=kOutput, calls=%fused_computation.4 | convolution fusion | flops 1573388032 | bytes 8729600 | tf_op jit(solution)/shard_map/dot_general | solution.py:39
  7.1 1.6 %copy.7 = f32[1024,256]{0,1:T(8,128)S(1)} copy(f32[1024,256]{1,0:T(8,128)} %get-tuple-element.6) | data formatting | bytes 2097152 | tf_op jit(solution)/shard_map/dot_general | solution.py:39
  8.7 0.1 fusion.2.white_ref
  8.8 0.0 copy-done.1
  8.8 38.2 %shard_map.55 = bf16[512,1024]{1,0:T(8,128)(2,1)S(1)} custom-call(s32[16]{0:T(128)S(1)} %copy-done.1, bf16[256,1024]{1,0:T(8,128)(2,1)S(1)} %fusion.2.white_ref), custom_call_target="tpu_custom_call" | custom-call | tf_op jit(solution)/shard_map/pallas_call | solution.py:740
  47.0 5.8 %multiply_convert_fusion = bf16[512,2048]{1,0:T(8,128)(2,1)} fusion(bf16[512,1024]{1,0:T(8,128)(2,1)S(1)} %shard_map.55, bf16[1024,2048]{1,0:T(8,128)(2,1)} %constant.14.clone), kind=kOutput, calls=%fused_computation | convolution fusion | flops 2149580800 | bytes 7340032 | tf_op jit(solution)/shard_map/dot_general | solution.py:810
  (1 shorter events, 0.0 us)
Async XLA Ops:
  0.0 1.4 %copy-start = (bf16[32,8,3000]{2,1,0:T(8,128)(2,1)S(1)}, bf16[32,8,3000]{2,1,0:T(8,128)(2,1)}, u32[]{:S(2)}) copy-start(bf16[32,8,3000]{2,1,0:T(8,128)(2,1)} %param.5) | copy-start | bytes 4608004
  1.4 7.4 %copy-start.1 = (s32[16]{0:T(128)S(1)}, s32[16]{0:T(128)}, u32[]{:S(2)}) copy-start(s32[16]{0:T(128)} %offsets_ref.1) | copy-start | bytes 196

commit v3 on v2

--- a/solution.py
+++ b/solution.py
@@ -458,11 +458,20 @@
         finishes(dz)
 
 
-def middle_kernel(shape, offsets_ref, white_ref, cross_ref, held, spec, made, back, joined,
-                  x_send, f_send, s_recv, r_send, r_recv):
+def middle_kernel(shape, offsets_hbm, mask_hbm, records_hbm, table_hbm, cross_ref,
+                  offsets_ref, mask_ref, records, table, spectrum, scale, white, held, spec, made, back, joined,
+                  l_sem, x_send, f_send, s_recv, r_send, r_recv):
     layers, wide, windows = shape
     pairs = offsets_ref.shape[0]
-    count = white_ref.shape[0] // windows
+    count = records.shape[0] // windows
+    chunks, width = table.shape[0], table.shape[2]
+    load = [pltpu.make_async_copy(records_hbm, records, l_sem.at[chunks])]
+    for n in range(chunks):
+        load.append(pltpu.make_async_copy(table_hbm.at[n], table.at[n], l_sem.at[n]))
+    load.append(pltpu.make_async_copy(offsets_hbm, offsets_ref, l_sem.at[chunks + 1]))
+    load.append(pltpu.make_async_copy(mask_hbm, mask_ref, l_sem.at[chunks + 2]))
+    for one in load:
+        one.start()
     parts = layers * wide
     pitch = spec.shape[0] // (2 * windows)
     half, top, last = layers // 2, layers - 1, parts - 1
@@ -508,6 +517,32 @@
     greet(me + wide, inner_high)
     replies_far = jnp.where(inner_low, wide, jnp.where(jnp.logical_and(inner_high, c == 1), 2 * wide - 1, 0))
     ships_there = jnp.where(jnp.logical_and(inner_low, near), 0, 1)
+
+    load[0].wait()
+    square = None
+    for n in range(chunks):
+        load[n + 1].wait()
+        part = jnp.dot(records[...], table[n], preferred_element_type=jnp.float32)
+        spectrum[:, n * width:(n + 1) * width] = part
+        for lane in range(0, width, LANES):
+            piece_square = part[:, lane:lane + LANES] * part[:, lane:lane + LANES]
+            square = piece_square if square is None else square + piece_square
+    power = jnp.sum(square, axis=1, keepdims=True) * (1.0 / (2 * F))
+    scale[...] = jnp.broadcast_to(lax.rsqrt(power + 1e-06), scale.shape)
+
+    for one in load[chunks + 1:]:
+        one.wait()
+    upper = lax.broadcasted_iota(jnp.int32, (2 * windows, LANES), 0) < windows
+
+    def whitening(i, carry):
+        rows = pl.ds(pl.multiple_of(i * 2 * windows, 2 * windows), 2 * windows)
+        alive = jnp.where(upper, mask_ref[2 * i].astype(jnp.float32), mask_ref[2 * i + 1].astype(jnp.float32))
+        gain = alive * scale[rows, :]
+        for x in range(2 * wide):
+            white[x, rows] = (spectrum[rows, x * LANES:(x + 1) * LANES] * gain).astype(jnp.bfloat16)
+        return carry
+
+    lax.fori_loop(0, count // 2, whitening, 0)
     pl.semaphore_wait(barrier, wide - 1 + replies_far + ships_there)
 
     def remote(source, target, send, recv, device):
@@ -517,7 +552,7 @@
         )
 
     def piece(ri, col):
-        return white_ref.at[:, pl.ds(pl.multiple_of((ri * wide + col) * LANES, LANES), LANES)]
+        return white.at[ri * wide + col]
 
     def swap(j, ri, col):
         return remote(piece(ri, col), held.at[me, ri], x_send.at[j, ri], s_recv.at[me, ri], first + col)
@@ -553,8 +588,7 @@
             lax.fori_loop(0, count // 2, one, 0, unroll=4)
 
     def own_rows(ri, i):
-        lanes = pl.ds(pl.multiple_of((ri * wide + q) * LANES, LANES), LANES)
-        return white_ref[pl.ds(pl.multiple_of(i * 2 * windows, 2 * windows), 2 * windows), lanes]
+        return white[ri * wide + q, pl.ds(pl.multiple_of(i * 2 * windows, 2 * windows), 2 * windows)]
 
     def take(s, onward=None):
         for ri in range(2):
@@ -732,25 +766,39 @@
     spans(0, first, low_begin, low_end, gave)
 
 
-def meet(layers, wide, white, windows, offsets):
+def meet(layers, wide, records, live_mask, offsets):
     pairs = offsets.shape[0]
-    count = white.shape[0] // windows
+    count, windows, length = records.shape
     parts = layers * wide
     pitch = (parts + 1) * count
+    rows = count * windows
+    width = 2 * LANES
+    chunks = 2 * F // width
+    table = np.ascontiguousarray(forward_table(length).reshape(length, chunks, width).transpose(1, 0, 2))
     return pl.pallas_call(
         functools.partial(middle_kernel, (layers, wide, windows)),
         out_shape=jax.ShapeDtypeStruct((count * pairs, 2 * F), jnp.bfloat16),
         in_specs=[
-            pl.BlockSpec(memory_space=pltpu.SMEM),
-            pl.BlockSpec(memory_space=pltpu.VMEM),
+            pl.BlockSpec(memory_space=pltpu.HBM),
+            pl.BlockSpec(memory_space=pltpu.HBM),
+            pl.BlockSpec(memory_space=pltpu.HBM),
+            pl.BlockSpec(memory_space=pltpu.HBM),
         ],
         out_specs=pl.BlockSpec(memory_space=pltpu.VMEM),
         scratch_shapes=[
-            pltpu.VMEM((parts, 2, count * windows, LANES), jnp.bfloat16),
+            pltpu.SMEM((pairs,), jnp.int32),
+            pltpu.SMEM((count,), jnp.int32),
+            pltpu.VMEM((rows, length), jnp.bfloat16),
+            pltpu.VMEM((chunks, length, width), jnp.bfloat16),
+            pltpu.VMEM((rows, 2 * F), jnp.float32),
+            pltpu.VMEM((rows, LANES), jnp.float32),
+            pltpu.VMEM((2 * wide, rows, LANES), jnp.bfloat16),
+            pltpu.VMEM((parts, 2, rows, LANES), jnp.bfloat16),
             pltpu.VMEM((2 * windows * pitch, LANES), jnp.float32),
             pltpu.VMEM((parts, pairs, 2, count, LANES), jnp.bfloat16),
             pltpu.VMEM((pairs, wide, 2, count, LANES), jnp.bfloat16),
             pltpu.VMEM((2 * wide * count * pairs, LANES), jnp.float32),
+            pltpu.SemaphoreType.DMA((chunks + 3,)),
             pltpu.SemaphoreType.DMA((wide - 1, 2)),
             pltpu.SemaphoreType.DMA((parts, 2)),
             pltpu.SemaphoreType.DMA((parts, 2)),
@@ -758,9 +806,9 @@
             pltpu.SemaphoreType.DMA((pairs, wide)),
         ],
         compiler_params=pltpu.CompilerParams(
-            vmem_limit_bytes=40 * 1024 * 1024, collective_id=1, has_side_effects=True
+            vmem_limit_bytes=36 * 1024 * 1024, collective_id=1, has_side_effects=True
         ),
-    )(offsets, white)
+    )(*[pltpu.with_memory_space_constraint(x, pltpu.HBM) for x in (offsets, live_mask, records.reshape(rows, length), jnp.asarray(table))])
 
 
 def shards(columns, records, live_mask, offsets):
@@ -772,14 +820,13 @@
     depth = min(layers - 1, (wide - 1 + reach) // wide)
     pieces = PIECES
     fold = columns == 2 and depth == layers - 1 and depth >= 2 and layers * wide == pairs and pairs * count == BAND
-    white = whiten(records, live_mask)
     if (
         columns == 2 and layers == 4 and layers * wide == pairs and pairs * count == BAND
         and F == wide * LANES and windows == 8 and count % 16 == 0
     ):
-        cross = meet(layers, wide, white, windows, offsets)
+        cross = meet(layers, wide, records, live_mask, offsets)
         return lags(cross, count, pairs, length)
-    spectra = white.reshape(count, windows * 8, LANES)
+    spectra = whiten(records, live_mask).reshape(count, windows * 8, LANES)
     slots = (depth + 1) * wide
     cross = pl.pallas_call(
         functools.partial(reach_kernel, (layers, columns, depth, pieces, windows, fold)),

time: 53.1 us -> 46.4 us (0.87)
  matrix products: 11.5 us -> 3.66 us
  Pallas kernels: 38.2 us -> 42.6 us
  local copies, waits for them, and re-layouts: 2.21 us -> 0.01 us
  other arithmetic: 0.91 us -> 0 us
    dot_general x1 -> x0, matrix products: 5.65 us -> none  [whiten(): jnp.dot(records.reshape(count * windows, length), jnp.asarray(forward_tab...]
    pallas_call x1, Pallas kernels: 38.2 us -> 42.6 us  [meet(): pl.pallas_call(functools.partial(middle_kernel, (layers, wide, windows)),...]
    dot_general x1, matrix products: 5.85 us -> 3.66 us  [lags(): jnp.dot(cross, jnp.asarray(inverse_table(length)), preferred_element_type...]
    dot_general x1 -> x0, local copies, waits for them, and re-layouts: 1.56 us -> none  [whiten(): jnp.dot(records.reshape(count * windows, length), jnp.asarray(forward_tab...]
    convert_element_type x2 -> x0, other arithmetic: 0.9 us -> none  [the longest x1 0.78 us: whiten(): gain = jnp.repeat(live_mask.astype(jnp.float32), windows)[:, None]]
where the time goes in v3:
time: 46.4 us; the launch traced here: 46.3 us
  Pallas kernels  42.6 us (92%)
  matrix products  3.66 us (8%)
    pallas_call x1, Pallas kernels, meet(): pl.pallas_call(functools.partial(middle_kernel, (layers, wide, windows)),...  42.6 us
    dot_general x1, matrix products, lags(): jnp.dot(cross, jnp.asarray(inverse_table(length)), preferred_element_type...  3.66 us

profile of v3, /device:TPU:0, one launch (start us, length us, event | category | flops | bytes accessed | tf_op | source)
XLA Modules:
  0.0 46.3 jit_solution(1658196452139512248)
XLA Ops:
  0.0 0.0 copy-start
  0.0 42.6 %shard_map.55 = bf16[512,1024]{1,0:T(8,128)(2,1)S(1)} custom-call(s32[16]{0:T(128)} %offsets_hbm.1, s32[32]{0:T(128)} %mask_hbm.1, bf16[256,3000]{1,0:T(8,128)(2,1)} %bitcast.4, bf16[4,3000,256]{2,1,0:T(8,128)(2,1)} %constant.6.clone.table_hbm), custom_call_target="tpu_custom_call" | custom-call | tf_op jit(solution)/shard_map/pallas_call | solution.py:778
  42.6 0.0 copy-done
  42.6 3.7 %multiply_convert_fusion = bf16[512,2048]{1,0:T(8,128)(2,1)} fusion(bf16[512,1024]{1,0:T(8,128)(2,1)S(1)} %shard_map.55, bf16[1024,2048]{1,0:T(8,128)(2,1)S(1)} %copy-done), kind=kOutput, calls=%fused_computation | convolution fusion | flops 2149580800 | bytes 7340032 | tf_op jit(solution)/shard_map/dot_general | solution.py:857
Async XLA Ops:
  0.0 42.6 %copy-start = (bf16[1024,2048]{1,0:T(8,128)(2,1)S(1)}, bf16[1024,2048]{1,0:T(8,128)(2,1)}, u32[]{:S(2)}) copy-start(bf16[1024,2048]{1,0:T(8,128)(2,1)} %constant.7.clone) | copy-start | bytes 12582916

commit v4 on v3

--- a/solution.py
+++ b/solution.py
@@ -460,7 +460,7 @@
 
 def middle_kernel(shape, offsets_hbm, mask_hbm, records_hbm, table_hbm, cross_ref,
                   offsets_ref, mask_ref, records, table, spectrum, scale, white, held, spec, made, back, joined,
-                  l_sem, x_send, f_send, s_recv, r_send, r_recv):
+                  l_sem, x_send, f_send, g_send, s_recv, r_send, r_recv):
     layers, wide, windows = shape
     pairs = offsets_ref.shape[0]
     count = records.shape[0] // windows
@@ -488,11 +488,9 @@
     neighbour = jnp.where(
         jnp.logical_or(z == 0, jnp.logical_and(inner_low, c == 1)), me + wide, me - wide)
     own_end = jnp.where(
-        z == 0, jnp.where(near, base, wide),
-        jnp.where(jnp.logical_and(inner_low, c == 1), base + wide, parts + 1))
+        z == 0, base, jnp.where(jnp.logical_and(inner_low, c == 1), base + wide, parts + 1))
     low_begin = jnp.where(
-        inner_low, jnp.where(near, base, wide),
-        jnp.where(jnp.logical_and(inner_high, c == 1), base + wide, 0))
+        inner_low, base, jnp.where(jnp.logical_and(inner_high, c == 1), base + wide, 0))
     low_end = jnp.where(
         inner_low, own_end, jnp.where(jnp.logical_and(inner_high, c == 1), parts + 1, 0))
 
@@ -563,6 +561,11 @@
     def ship(s, ri):
         return remote(held.at[s, ri], held.at[s, ri], f_send.at[s, ri], s_recv.at[s, ri], neighbour)
 
+    both_ways = jnp.logical_and(inner_low, c == 1)
+
+    def drop(s, ri, source):
+        return remote(source, held.at[s, ri], g_send.at[s, ri], s_recv.at[s, ri], me - wide)
+
     def reply(d, k):
         return remote(made.at[d, k], back.at[k, q], r_send.at[d, k], r_recv.at[k, q], d)
 
@@ -571,6 +574,11 @@
 
     for ri in range(2):
         ship_own(ri).start()
+
+    @pl.when(both_ways)
+    def _():
+        for ri in range(2):
+            drop(me, ri, piece(ri, q)).start()
     columns = (sib_q, mate_q, far_q)
     for j, col in enumerate(columns):
         for ri in range(2):
@@ -590,7 +598,7 @@
     def own_rows(ri, i):
         return white[ri * wide + q, pl.ds(pl.multiple_of(i * 2 * windows, 2 * windows), 2 * windows)]
 
-    def take(s, onward=None):
+    def take(s, onward=None, downward=None):
         for ri in range(2):
             ship(s, ri).wait_recv()
         if onward is not None:
@@ -598,6 +606,11 @@
             def _():
                 for ri in range(2):
                     ship(s, ri).start()
+        if downward is not None:
+            @pl.when(downward)
+            def _():
+                for ri in range(2):
+                    drop(s, ri, held.at[s, ri]).start()
         settle(s, lambda ri, i: held[s, ri, pl.ds(pl.multiple_of(i * 2 * windows, 2 * windows), 2 * windows)])
 
     def block(d, k):
@@ -660,10 +673,10 @@
 
     settle(me, own_rows)
     for col in columns:
-        take(first + col, z >= 0)
+        take(first + col, z >= 0, both_ways)
     blocks(first, first + wide, first + 1, first + wide + jnp.where(z == top, 1, 0))
 
-    @pl.when(jnp.logical_and(z == 0, near))
+    @pl.when(z == 0)
     def _():
         for group, reached in ((pair_1, reached_1), (pair_2, reached_2)):
             for col in group:
@@ -679,13 +692,10 @@
         lower(pair_1)
         for col in pair_1:
             take(base + col)
+        blocks(2 * y, 2 * y + 2, *reached_1(base))
         blocks(wide, base, *reached_1(base))
         lower(pair_2)
-        blocks(0, wide, *reached_1(base))
-
-        @pl.when(jnp.logical_not(near))
-        def _():
-            blocks(0, wide, wide, base)
+        blocks(2 - 2 * y, wide - 2 * y, *reached_1(base))
         for col in pair_2:
             take(base + col)
         blocks(0, base, *reached_2(base))
@@ -708,9 +718,14 @@
         def _():
             for col in pair_1 + pair_2:
                 take(wide + col)
-            for col in pair_1 + pair_2:
+            spans(wide, base, top * wide, parts + 1, block)
+            for col in pair_1:
                 take(col)
-            blocks(0, base, top * wide, parts + 1)
+            blocks(2 * y, 2 * y + 2, top * wide, parts + 1)
+            for col in pair_2:
+                take(col)
+            blocks(2 - 2 * y, wide - 2 * y, top * wide, parts + 1)
+            spans(wide, base, top * wide, parts + 1, give)
 
     def unpack(source, k, col):
         for ri in range(2):
@@ -756,6 +771,15 @@
         return carry
 
     lax.fori_loop(first, first + wide, sent, 0)
+
+    @pl.when(both_ways)
+    def _():
+        def dropped(s, carry):
+            for ri in range(2):
+                drop(s, ri, held.at[s, ri]).wait_send()
+            return carry
+
+        lax.fori_loop(first, first + wide, dropped, 0)
 
     @pl.when(jnp.logical_or(jnp.logical_and(inner_low, c == 1), jnp.logical_and(inner_high, near)))
     def _():
@@ -800,6 +824,7 @@
             pltpu.VMEM((2 * wide * count * pairs, LANES), jnp.float32),
             pltpu.SemaphoreType.DMA((chunks + 3,)),
             pltpu.SemaphoreType.DMA((wide - 1, 2)),
+            pltpu.SemaphoreType.DMA((parts, 2)),
             pltpu.SemaphoreType.DMA((parts, 2)),
             pltpu.SemaphoreType.DMA((parts, 2)),
             pltpu.SemaphoreType.DMA((parts, pairs)),

time: 46.4 us -> 44.5 us (0.959)
  Pallas kernels: 42.6 us -> 40.7 us
    pallas_call x1, Pallas kernels: 42.6 us -> 40.7 us  [meet(): pl.pallas_call(functools.partial(middle_kernel, (layers, wide, windows)),...]
where the time goes in v4:
time: 44.5 us; the launch traced here: 44.4 us
  Pallas kernels  40.7 us (91%)
  matrix products  3.66 us (8%)
    pallas_call x1, Pallas kernels, meet(): pl.pallas_call(functools.partial(middle_kernel, (layers, wide, windows)),...  40.7 us
    dot_general x1, matrix products, lags(): jnp.dot(cross, jnp.asarray(inverse_table(length)), preferred_element_type...  3.66 us

profile of v4, /device:TPU:0, one launch (start us, length us, event | category | flops | bytes accessed | tf_op | source)
XLA Modules:
  0.0 44.4 jit_solution(11083589577388547419)
XLA Ops:
  0.0 0.0 copy-start
  0.0 40.7 %shard_map.55 = bf16[512,1024]{1,0:T(8,128)(2,1)S(1)} custom-call(s32[16]{0:T(128)} %offsets_hbm.1, s32[32]{0:T(128)} %mask_hbm.1, bf16[256,3000]{1,0:T(8,128)(2,1)} %bitcast.4, bf16[4,3000,256]{2,1,0:T(8,128)(2,1)} %constant.6.clone.table_hbm), custom_call_target="tpu_custom_call" | custom-call | tf_op jit(solution)/shard_map/pallas_call | solution.py:802
  40.7 0.0 copy-done
  40.7 3.7 %multiply_convert_fusion = bf16[512,2048]{1,0:T(8,128)(2,1)} fusion(bf16[512,1024]{1,0:T(8,128)(2,1)S(1)} %shard_map.55, bf16[1024,2048]{1,0:T(8,128)(2,1)S(1)} %copy-done), kind=kOutput, calls=%fused_computation | convolution fusion | flops 2149580800 | bytes 7340032 | tf_op jit(solution)/shard_map/dot_general | solution.py:882
Async XLA Ops:
  0.0 40.7 %copy-start = (bf16[1024,2048]{1,0:T(8,128)(2,1)S(1)}, bf16[1024,2048]{1,0:T(8,128)(2,1)}, u32[]{:S(2)}) copy-start(bf16[1024,2048]{1,0:T(8,128)(2,1)} %constant.7.clone) | copy-start | bytes 12582916

commit v5 on v4

--- a/solution.py
+++ b/solution.py
@@ -489,11 +489,6 @@
         jnp.logical_or(z == 0, jnp.logical_and(inner_low, c == 1)), me + wide, me - wide)
     own_end = jnp.where(
         z == 0, base, jnp.where(jnp.logical_and(inner_low, c == 1), base + wide, parts + 1))
-    low_begin = jnp.where(
-        inner_low, base, jnp.where(jnp.logical_and(inner_high, c == 1), base + wide, 0))
-    low_end = jnp.where(
-        inner_low, own_end, jnp.where(jnp.logical_and(inner_high, c == 1), parts + 1, 0))
-
     barrier = pltpu.get_barrier_semaphore()
 
     def greet(device, condition):
@@ -552,25 +547,31 @@
     def piece(ri, col):
         return white.at[ri * wide + col]
 
-    def swap(j, ri, col):
-        return remote(piece(ri, col), held.at[me, ri], x_send.at[j, ri], s_recv.at[me, ri], first + col)
+    def swap(ri, col):
+        return remote(piece(ri, col), held.at[me, ri], x_send, s_recv.at[me], first + col)
 
     def ship_own(ri):
-        return remote(piece(ri, q), held.at[me, ri], f_send.at[me, ri], s_recv.at[me, ri], neighbour)
-
-    def ship(s, ri):
-        return remote(held.at[s, ri], held.at[s, ri], f_send.at[s, ri], s_recv.at[s, ri], neighbour)
+        return remote(piece(ri, q), held.at[me, ri], f_send, s_recv.at[me], neighbour)
+
+    def ship(s):
+        return remote(held.at[s], held.at[s], f_send, s_recv.at[s], neighbour)
 
     both_ways = jnp.logical_and(inner_low, c == 1)
 
-    def drop(s, ri, source):
-        return remote(source, held.at[s, ri], g_send.at[s, ri], s_recv.at[s, ri], me - wide)
+    def drop_own(ri):
+        return remote(piece(ri, q), held.at[me, ri], g_send, s_recv.at[me], me - wide)
+
+    def drop(s):
+        return remote(held.at[s], held.at[s], g_send, s_recv.at[s], me - wide)
+
+    def made_at(d, k):
+        return made.at[d * pairs + k]
 
     def reply(d, k):
-        return remote(made.at[d, k], back.at[k, q], r_send.at[d, k], r_recv.at[k, q], d)
-
-    def replied(k, col):
-        return remote(back.at[k, col], back.at[k, col], r_send.at[me, k], r_recv.at[k, col], me)
+        return remote(made_at(d, k), back.at[k, q], r_send, r_recv.at[k], d)
+
+    def shipped(slots, send):
+        remote(held.at[0:slots], held.at[0:slots], send, s_recv.at[0], neighbour).wait_send()
 
     for ri in range(2):
         ship_own(ri).start()
@@ -578,11 +579,11 @@
     @pl.when(both_ways)
     def _():
         for ri in range(2):
-            drop(me, ri, piece(ri, q)).start()
+            drop_own(ri).start()
     columns = (sib_q, mate_q, far_q)
-    for j, col in enumerate(columns):
+    for col in columns:
         for ri in range(2):
-            swap(j, ri, col).start()
+            swap(ri, col).start()
 
     def settle(s, load):
         for ri in range(2):
@@ -599,18 +600,15 @@
         return white[ri * wide + q, pl.ds(pl.multiple_of(i * 2 * windows, 2 * windows), 2 * windows)]
 
     def take(s, onward=None, downward=None):
-        for ri in range(2):
-            ship(s, ri).wait_recv()
+        ship(s).wait_recv()
         if onward is not None:
             @pl.when(onward)
             def _():
-                for ri in range(2):
-                    ship(s, ri).start()
+                ship(s).start()
         if downward is not None:
             @pl.when(downward)
             def _():
-                for ri in range(2):
-                    drop(s, ri, held.at[s, ri]).start()
+                drop(s).start()
         settle(s, lambda ri, i: held[s, ri, pl.ds(pl.multiple_of(i * 2 * windows, 2 * windows), 2 * windows)])
 
     def block(d, k):
@@ -626,8 +624,8 @@
                 re, im = cr * pr + ci * pi, ci * pr - cr * pi
                 real, imag = (re, im) if w == 0 else (real + re, imag + im)
             rows = slice(g * 16, g * 16 + 16)
-            made[d, k, 0, rows] = (real * (1.0 / windows)).astype(jnp.bfloat16)
-            made[d, k, 1, rows] = (imag * (1.0 / windows)).astype(jnp.bfloat16)
+            made[d * pairs + k, 0, rows] = (real * (1.0 / windows)).astype(jnp.bfloat16)
+            made[d * pairs + k, 1, rows] = (imag * (1.0 / windows)).astype(jnp.bfloat16)
 
     def spans(d_begin, d_end, u_begin, u_end, visit):
         def reach(u, carry):
@@ -643,11 +641,6 @@
         @pl.when(d != me)
         def _():
             reply(d, k).start()
-
-    def gave(d, k):
-        @pl.when(d != me)
-        def _():
-            reply(d, k).wait_send()
 
     def blocks(*span):
         spans(*span, block)
@@ -737,16 +730,26 @@
 
     def collect(k, carry):
         away = me + k + 1 >= own_end
+        def received(cols):
+            remote(back.at[k, 0:cols], back.at[k, 0:cols], r_send, r_recv.at[k], me).wait_recv()
+
+        @pl.when(away)
+        def _():
+            received(wide)
+
+        @pl.when(jnp.logical_not(away))
+        def _():
+            received(wide - 1)
+
         for col in range(wide):
             here = jnp.logical_and(q == col, jnp.logical_not(away))
 
             @pl.when(here)
             def _():
-                unpack(made.at[me, k], k, col)
+                unpack(made_at(me, k), k, col)
 
             @pl.when(jnp.logical_not(here))
             def _():
-                replied(k, col).wait_recv()
                 unpack(back.at[k, col], k, col)
         return carry
 
@@ -761,33 +764,34 @@
 
     lax.fori_loop(0, count * pairs // 16, pack, 0, unroll=2)
 
-    for j, col in enumerate(columns):
-        for ri in range(2):
-            swap(j, ri, col).wait_send()
-
-    def sent(s, carry):
-        for ri in range(2):
-            ship(s, ri).wait_send()
-        return carry
-
-    lax.fori_loop(first, first + wide, sent, 0)
+    shipped(wide - 1, x_send)
+    forwards = jnp.logical_or(both_ways, jnp.logical_and(inner_high, near))
+
+    @pl.when(forwards)
+    def _():
+        shipped(2 * wide, f_send)
+
+    @pl.when(jnp.logical_not(forwards))
+    def _():
+        shipped(wide, f_send)
 
     @pl.when(both_ways)
     def _():
-        def dropped(s, carry):
-            for ri in range(2):
-                drop(s, ri, held.at[s, ri]).wait_send()
-            return carry
-
-        lax.fori_loop(first, first + wide, dropped, 0)
-
-    @pl.when(jnp.logical_or(jnp.logical_and(inner_low, c == 1), jnp.logical_and(inner_high, near)))
-    def _():
-        begin = jnp.where(inner_low, 0, top * wide)
-        lax.fori_loop(begin, begin + wide, sent, 0)
-
-    spans(first, first + wide, first + 1, own_end, gave)
-    spans(0, first, low_begin, low_end, gave)
+        shipped(wide, g_send)
+
+    for i in range(parts):
+        layer, odd = i // wide, i % 2 == 1
+        ends = base if layer == 0 else base + wide if layer == half - 1 and odd else parts + 1
+        replies = sum(
+            min(ends, d + pairs + 1) - d - 1 for d in range(layer * wide, (layer + 1) * wide) if d != i)
+        if layer == half - 1 or (layer == half and odd):
+            begins = base if layer == half - 1 else base + wide
+            replies += sum(min(ends, d + pairs + 1) - begins for d in range(layer * wide))
+
+        @pl.when(me == i)
+        def _():
+            done = made.at[0:replies]
+            remote(done, done, r_send, r_recv.at[0], me).wait_send()
 
 
 def meet(layers, wide, records, live_mask, offsets):
@@ -819,16 +823,16 @@
             pltpu.VMEM((2 * wide, rows, LANES), jnp.bfloat16),
             pltpu.VMEM((parts, 2, rows, LANES), jnp.bfloat16),
             pltpu.VMEM((2 * windows * pitch, LANES), jnp.float32),
-            pltpu.VMEM((parts, pairs, 2, count, LANES), jnp.bfloat16),
+            pltpu.VMEM((parts * pairs, 2, count, LANES), jnp.bfloat16),
             pltpu.VMEM((pairs, wide, 2, count, LANES), jnp.bfloat16),
             pltpu.VMEM((2 * wide * count * pairs, LANES), jnp.float32),
             pltpu.SemaphoreType.DMA((chunks + 3,)),
-            pltpu.SemaphoreType.DMA((wide - 1, 2)),
-            pltpu.SemaphoreType.DMA((parts, 2)),
-            pltpu.SemaphoreType.DMA((parts, 2)),
-            pltpu.SemaphoreType.DMA((parts, 2)),
-            pltpu.SemaphoreType.DMA((parts, pairs)),
-            pltpu.SemaphoreType.DMA((pairs, wide)),
+            pltpu.SemaphoreType.DMA,
+            pltpu.SemaphoreType.DMA,
+            pltpu.SemaphoreType.DMA,
+            pltpu.SemaphoreType.DMA((parts,)),
+            pltpu.SemaphoreType.DMA,
+            pltpu.SemaphoreType.DMA((pairs,)),
         ],
         compiler_params=pltpu.CompilerParams(
             vmem_limit_bytes=36 * 1024 * 1024, collective_id=1, has_side_effects=True

time: 44.5 us -> 40.7 us (0.915)
  Pallas kernels: 40.7 us -> 36.9 us
    pallas_call x1, Pallas kernels: 40.7 us -> 36.9 us  [meet(): pl.pallas_call(functools.partial(middle_kernel, (layers, wide, windows)),...]
where the time goes in v5:
time: 40.7 us; the launch traced here: 40.5 us
  Pallas kernels  36.9 us (91%)
  matrix products  3.66 us (9%)
    pallas_call x1, Pallas kernels, meet(): pl.pallas_call(functools.partial(middle_kernel, (layers, wide, windows)),...  36.9 us
    dot_general x1, matrix products, lags(): jnp.dot(cross, jnp.asarray(inverse_table(length)), preferred_element_type...  3.66 us

profile of v5, /device:TPU:0, one launch (start us, length us, event | category | flops | bytes accessed | tf_op | source)
XLA Modules:
  0.0 40.5 jit_solution(5733777775958953218)
XLA Ops:
  0.0 0.0 copy-start
  0.0 36.9 %shard_map.55 = bf16[512,1024]{1,0:T(8,128)(2,1)S(1)} custom-call(s32[16]{0:T(128)} %offsets_hbm.1, s32[32]{0:T(128)} %mask_hbm.1, bf16[256,3000]{1,0:T(8,128)(2,1)} %bitcast.4, bf16[4,3000,256]{2,1,0:T(8,128)(2,1)} %constant.6.clone.table_hbm), custom_call_target="tpu_custom_call" | custom-call | tf_op jit(solution)/shard_map/pallas_call | solution.py:806
  36.9 0.0 copy-done
  36.9 3.7 %multiply_convert_fusion = bf16[512,2048]{1,0:T(8,128)(2,1)} fusion(bf16[512,1024]{1,0:T(8,128)(2,1)S(1)} %shard_map.55, bf16[1024,2048]{1,0:T(8,128)(2,1)S(1)} %copy-done), kind=kOutput, calls=%fused_computation | convolution fusion | flops 2149580800 | bytes 7340032 | tf_op jit(solution)/shard_map/dot_general | solution.py:886
Async XLA Ops:
  0.0 36.9 %copy-start = (bf16[1024,2048]{1,0:T(8,128)(2,1)S(1)}, bf16[1024,2048]{1,0:T(8,128)(2,1)}, u32[]{:S(2)}) copy-start(bf16[1024,2048]{1,0:T(8,128)(2,1)} %constant.7.clone) | copy-start | bytes 12582916

commit v6 on v5

--- a/solution.py
+++ b/solution.py
@@ -13,6 +13,7 @@
 F0 = 6
 LAGS = 2048
 LANES = 128
+SPAN = 512
 BAND = 512
 PIECES = 4
 LAYER_CHIPS = 4
@@ -458,8 +459,8 @@
         finishes(dz)
 
 
-def middle_kernel(shape, offsets_hbm, mask_hbm, records_hbm, table_hbm, cross_ref,
-                  offsets_ref, mask_ref, records, table, spectrum, scale, white, held, spec, made, back, joined,
+def middle_kernel(shape, offsets_hbm, mask_hbm, records_hbm, table_hbm, inverse_hbm, half_ref, cross_ref, inverse,
+                  offsets_ref, mask_ref, records, table, crossed, spectrum, white, held, spec, made, back, joined,
                   l_sem, x_send, f_send, g_send, s_recv, r_send, r_recv):
     layers, wide, windows = shape
     pairs = offsets_ref.shape[0]
@@ -512,30 +513,30 @@
     ships_there = jnp.where(jnp.logical_and(inner_low, near), 0, 1)
 
     load[0].wait()
-    square = None
     for n in range(chunks):
         load[n + 1].wait()
-        part = jnp.dot(records[...], table[n], preferred_element_type=jnp.float32)
-        spectrum[:, n * width:(n + 1) * width] = part
-        for lane in range(0, width, LANES):
-            piece_square = part[:, lane:lane + LANES] * part[:, lane:lane + LANES]
-            square = piece_square if square is None else square + piece_square
-    power = jnp.sum(square, axis=1, keepdims=True) * (1.0 / (2 * F))
-    scale[...] = jnp.broadcast_to(lax.rsqrt(power + 1e-06), scale.shape)
-
+        spectrum[:, n * width:(n + 1) * width] = jnp.dot(
+            records[...], table[n], preferred_element_type=jnp.float32)
     for one in load[chunks + 1:]:
         one.wait()
-    upper = lax.broadcasted_iota(jnp.int32, (2 * windows, LANES), 0) < windows
+    upper = lax.broadcasted_iota(jnp.int32, (2 * windows, 1), 0) < windows
 
     def whitening(i, carry):
         rows = pl.ds(pl.multiple_of(i * 2 * windows, 2 * windows), 2 * windows)
+        values = [spectrum[rows, x * LANES:(x + 1) * LANES] for x in range(2 * wide)]
+        square = values[0] * values[0]
+        for value in values[1:]:
+            square += value * value
+        power = jnp.sum(square, axis=1, keepdims=True) * (1.0 / (2 * F))
         alive = jnp.where(upper, mask_ref[2 * i].astype(jnp.float32), mask_ref[2 * i + 1].astype(jnp.float32))
-        gain = alive * scale[rows, :]
-        for x in range(2 * wide):
-            white[x, rows] = (spectrum[rows, x * LANES:(x + 1) * LANES] * gain).astype(jnp.bfloat16)
+        gain = alive * lax.rsqrt(power + 1e-06)
+        for x, value in enumerate(values):
+            white[x, rows] = (value * gain).astype(jnp.bfloat16)
         return carry
 
-    lax.fori_loop(0, count // 2, whitening, 0)
+    lax.fori_loop(0, count // 2, whitening, 0, unroll=4)
+    fetch = pltpu.make_async_copy(inverse_hbm, inverse, l_sem.at[0])
+    fetch.start()
     pl.semaphore_wait(barrier, wide - 1 + replies_far + ships_there)
 
     def remote(source, target, send, recv, device):
@@ -720,13 +721,16 @@
             blocks(2 - 2 * y, wide - 2 * y, top * wide, parts + 1)
             spans(wide, base, top * wide, parts + 1, give)
 
+    group = pairs // 2
+
     def unpack(source, k, col):
         for ri in range(2):
             for g in range(count // 16):
                 value = source[ri, g * 16:g * 16 + 16].astype(jnp.float32)
                 for part in range(2):
-                    row = (ri * wide + col) * count * pairs + (g * 16 + part * 8) * pairs + k
-                    joined[pl.ds(row, 8, stride=pairs), :] = value[part * 8:part * 8 + 8]
+                    seg = (k // group) * 2 * wide + ri * wide + col
+                    row = (seg * count + g * 16 + part * 8) * group + k % group
+                    joined[pl.ds(row, 8, stride=group), :] = value[part * 8:part * 8 + 8]
 
     def collect(k, carry):
         away = me + k + 1 >= own_end
@@ -753,16 +757,24 @@
                 unpack(back.at[k, col], k, col)
         return carry
 
-    lax.fori_loop(0, parts - me, collect, 0)
-
-    def pack(i, carry):
-        rows = pl.ds(pl.multiple_of(i * 16, 16), 16)
-        for x in range(2 * wide):
-            start = pl.multiple_of(x * count * pairs + i * 16, 16)
-            cross_ref[rows, x * LANES:(x + 1) * LANES] = joined[pl.ds(start, 16), :].astype(jnp.bfloat16)
-        return carry
-
-    lax.fori_loop(0, count * pairs // 16, pack, 0, unroll=2)
+    def pack(which, target):
+        def one(i, carry):
+            rows = pl.ds(pl.multiple_of(i * 16, 16), 16)
+            for x in range(2 * wide):
+                start = pl.multiple_of((which * 2 * wide + x) * count * group + i * 16, 16)
+                target[rows, x * LANES:(x + 1) * LANES] = joined[pl.ds(start, 16), :].astype(jnp.bfloat16)
+            return carry
+
+        lax.fori_loop(0, count * group // 16, one, 0, unroll=2)
+
+    lax.fori_loop(0, jnp.minimum(group, parts - me), collect, 0)
+    pack(0, crossed)
+    fetch.wait()
+    for n in range(0, LAGS, SPAN):
+        lagged = jnp.dot(crossed[...], inverse[:, n:n + SPAN], preferred_element_type=jnp.float32)
+        half_ref[:, n:n + SPAN] = (lagged * (1.0 / math.sqrt(F))).astype(jnp.bfloat16)
+    lax.fori_loop(group, parts - me, collect, 0)
+    pack(1, cross_ref)
 
     shipped(wide - 1, x_send)
     forwards = jnp.logical_or(both_ways, jnp.logical_and(inner_high, near))
@@ -805,21 +817,26 @@
     table = np.ascontiguousarray(forward_table(length).reshape(length, chunks, width).transpose(1, 0, 2))
     return pl.pallas_call(
         functools.partial(middle_kernel, (layers, wide, windows)),
-        out_shape=jax.ShapeDtypeStruct((count * pairs, 2 * F), jnp.bfloat16),
+        out_shape=[
+            jax.ShapeDtypeStruct((count * pairs // 2, LAGS), jnp.bfloat16),
+            jax.ShapeDtypeStruct((count * pairs // 2, 2 * F), jnp.bfloat16),
+            jax.ShapeDtypeStruct((2 * F, LAGS), jnp.bfloat16),
+        ],
         in_specs=[
             pl.BlockSpec(memory_space=pltpu.HBM),
             pl.BlockSpec(memory_space=pltpu.HBM),
             pl.BlockSpec(memory_space=pltpu.HBM),
             pl.BlockSpec(memory_space=pltpu.HBM),
+            pl.BlockSpec(memory_space=pltpu.HBM),
         ],
-        out_specs=pl.BlockSpec(memory_space=pltpu.VMEM),
+        out_specs=[pl.BlockSpec(memory_space=pltpu.VMEM)] * 3,
         scratch_shapes=[
             pltpu.SMEM((pairs,), jnp.int32),
             pltpu.SMEM((count,), jnp.int32),
             pltpu.VMEM((rows, length), jnp.bfloat16),
             pltpu.VMEM((chunks, length, width), jnp.bfloat16),
+            pltpu.VMEM((count * pairs // 2, 2 * F), jnp.bfloat16),
             pltpu.VMEM((rows, 2 * F), jnp.float32),
-            pltpu.VMEM((rows, LANES), jnp.float32),
             pltpu.VMEM((2 * wide, rows, LANES), jnp.bfloat16),
             pltpu.VMEM((parts, 2, rows, LANES), jnp.bfloat16),
             pltpu.VMEM((2 * windows * pitch, LANES), jnp.float32),
@@ -837,7 +854,40 @@
         compiler_params=pltpu.CompilerParams(
             vmem_limit_bytes=36 * 1024 * 1024, collective_id=1, has_side_effects=True
         ),
-    )(*[pltpu.with_memory_space_constraint(x, pltpu.HBM) for x in (offsets, live_mask, records.reshape(rows, length), jnp.asarray(table))])
+    )(*[
+        pltpu.with_memory_space_constraint(x, pltpu.HBM)
+        for x in (offsets, live_mask, records.reshape(rows, length), jnp.asarray(table),
+                  jnp.asarray(inverse_table(length)))
+    ])
+
+
+def finish_kernel(half_ref, cross_ref, table_ref, out_hbm, stage, sem):
+    group = out_hbm.shape[1] // 2
+    copies = [pltpu.make_async_copy(half_ref, out_hbm.at[:, 0:group], sem.at[0])]
+    copies[0].start()
+    for i, n in enumerate(range(0, LAGS, SPAN)):
+        lagged = jnp.dot(cross_ref[...], table_ref[:, n:n + SPAN], preferred_element_type=jnp.float32)
+        lagged = (lagged * (1.0 / math.sqrt(F))).astype(jnp.bfloat16)
+        stage[:, :, n:n + SPAN] = lagged.reshape(stage.shape[0], group, SPAN)
+        copies.append(pltpu.make_async_copy(
+            stage.at[:, :, n:n + SPAN], out_hbm.at[:, group:2 * group, n:n + SPAN], sem.at[i + 1]))
+        copies[-1].start()
+    for one in copies:
+        one.wait()
+
+
+def finish(half, cross, table, count, pairs):
+    return pl.pallas_call(
+        finish_kernel,
+        out_shape=jax.ShapeDtypeStruct((count, pairs, LAGS), jnp.bfloat16),
+        in_specs=[pl.BlockSpec(memory_space=pltpu.VMEM)] * 3,
+        out_specs=pl.BlockSpec(memory_space=pltpu.HBM),
+        scratch_shapes=[
+            pltpu.VMEM((count, pairs // 2, LAGS), jnp.bfloat16),
+            pltpu.SemaphoreType.DMA((LAGS // SPAN + 1,)),
+        ],
+        compiler_params=pltpu.CompilerParams(vmem_limit_bytes=16 * 1024 * 1024),
+    )(half.reshape(count, pairs // 2, LAGS), cross, table)
 
 
 def shards(columns, records, live_mask, offsets):
@@ -853,8 +903,8 @@
         columns == 2 and layers == 4 and layers * wide == pairs and pairs * count == BAND
         and F == wide * LANES and windows == 8 and count % 16 == 0
     ):
-        cross = meet(layers, wide, records, live_mask, offsets)
-        return lags(cross, count, pairs, length)
+        half, cross, inverse = meet(layers, wide, records, live_mask, offsets)
+        return finish(half, cross, inverse, count, pairs)
     spectra = whiten(records, live_mask).reshape(count, windows * 8, LANES)
     slots = (depth + 1) * wide
     cross = pl.pallas_call(

time: 40.7 us -> 38.9 us (0.956)
  matrix products: 3.66 us -> 0 us
  Pallas kernels: 36.9 us -> 38.8 us
    dot_general x1 -> x0, matrix products: 3.66 us -> none  [lags(): jnp.dot(cross, jnp.asarray(inverse_table(length)), preferred_element_type...]
    pallas_call x0 -> x1, Pallas kernels: none -> 2 us  [finish(): pl.pallas_call(finish_kernel, out_shape=jax.ShapeDtypeStruct((count, pair...]
where the time goes in v6:
time: 38.9 us; the launch traced here: 38.8 us
  Pallas kernels  38.8 us (100%)
    pallas_call x1, Pallas kernels, meet(): pl.pallas_call(functools.partial(middle_kernel, (layers, wide, windows)),...  36.8 us
    pallas_call x1, Pallas kernels, finish(): pl.pallas_call(finish_kernel, out_shape=jax.ShapeDtypeStruct((count, pair...  2 us

profile of v6, /device:TPU:0, one launch (start us, length us, event | category | flops | bytes accessed | tf_op | source)
XLA Modules:
  0.0 38.8 jit_solution(9198575319549570398)
XLA Ops:
  0.0 36.8 %shard_map.55 = (bf16[256,2048]{1,0:T(8,128)(2,1)S(1)}, bf16[256,1024]{1,0:T(8,128)(2,1)S(1)}, bf16[1024,2048]{1,0:T(8,128)(2,1)S(1)}) custom-call(s32[16]{0:T(128)} %offsets_hbm.1, s32[32]{0:T(128)} %mask_hbm.1, bf16[256,3000]{1,0:T(8,128)(2,1)} %bitcast.3, bf16[4,3000,256]{2,1,0:T(8,128)(2,1)} %constant.4.clone.table_hbm, ...), custom_call_target="tpu_custom_call" | custom-call | tf_op jit(solution)/shard_map/pallas_call | solution.py:818
  36.8 2.0 %shard_map.56 = bf16[32,16,2048]{2,1,0:T(8,128)(2,1)} custom-call(bf16[32,8,2048]{2,1,0:T(8,128)(2,1)S(1)} %bitcast.2, bf16[256,1024]{1,0:T(8,128)(2,1)S(1)} %get-tuple-element.9.cross_ref, bf16[1024,2048]{1,0:T(8,128)(2,1)S(1)} %get-tuple-element.10.table_ref), custom_call_target="tpu_custom_call" | custom-call | tf_op jit(solution)/shard_map/pallas_call | solution.py:880

commit v7 on v6

--- a/solution.py
+++ b/solution.py
@@ -513,17 +513,21 @@
     ships_there = jnp.where(jnp.logical_and(inner_low, near), 0, 1)
 
     load[0].wait()
-    for n in range(chunks):
-        load[n + 1].wait()
-        spectrum[:, n * width:(n + 1) * width] = jnp.dot(
-            records[...], table[n], preferred_element_type=jnp.float32)
+    def transform(n, carry):
+        pltpu.make_async_copy(table_hbm.at[n], table.at[n], l_sem.at[n]).wait()
+        spectrum[n] = jnp.dot(records[...], table[n], preferred_element_type=jnp.float32)
+        return carry
+
+    lax.fori_loop(0, chunks, transform, 0)
     for one in load[chunks + 1:]:
         one.wait()
     upper = lax.broadcasted_iota(jnp.int32, (2 * windows, 1), 0) < windows
 
     def whitening(i, carry):
         rows = pl.ds(pl.multiple_of(i * 2 * windows, 2 * windows), 2 * windows)
-        values = [spectrum[rows, x * LANES:(x + 1) * LANES] for x in range(2 * wide)]
+        values = [
+            spectrum[x * LANES // width, rows, x * LANES % width:x * LANES % width + LANES]
+            for x in range(2 * wide)]
         square = values[0] * values[0]
         for value in values[1:]:
             square += value * value
@@ -770,9 +774,14 @@
     lax.fori_loop(0, jnp.minimum(group, parts - me), collect, 0)
     pack(0, crossed)
     fetch.wait()
-    for n in range(0, LAGS, SPAN):
-        lagged = jnp.dot(crossed[...], inverse[:, n:n + SPAN], preferred_element_type=jnp.float32)
-        half_ref[:, n:n + SPAN] = (lagged * (1.0 / math.sqrt(F))).astype(jnp.bfloat16)
+
+    def invert(n, carry):
+        span = pl.ds(pl.multiple_of(n * SPAN, SPAN), SPAN)
+        lagged = jnp.dot(crossed[...], inverse[:, span], preferred_element_type=jnp.float32)
+        half_ref[:, span] = (lagged * (1.0 / math.sqrt(F))).astype(jnp.bfloat16)
+        return carry
+
+    lax.fori_loop(0, LAGS // SPAN, invert, 0)
     lax.fori_loop(group, parts - me, collect, 0)
     pack(1, cross_ref)
 
@@ -836,7 +845,7 @@
             pltpu.VMEM((rows, length), jnp.bfloat16),
             pltpu.VMEM((chunks, length, width), jnp.bfloat16),
             pltpu.VMEM((count * pairs // 2, 2 * F), jnp.bfloat16),
-            pltpu.VMEM((rows, 2 * F), jnp.float32),
+            pltpu.VMEM((chunks, rows, width), jnp.float32),
             pltpu.VMEM((2 * wide, rows, LANES), jnp.bfloat16),
             pltpu.VMEM((parts, 2, rows, LANES), jnp.bfloat16),
             pltpu.VMEM((2 * windows * pitch, LANES), jnp.float32),

time: 38.9 us -> 37.5 us (0.964)
  Pallas kernels: 38.8 us -> 37.3 us
    pallas_call x1, Pallas kernels: 36.8 us -> 35.3 us  [meet(): pl.pallas_call(functools.partial(middle_kernel, (layers, wide, windows)),...]
where the time goes in v7:
time: 37.5 us; the launch traced here: 37.3 us
  Pallas kernels  37.3 us (99%)
    pallas_call x1, Pallas kernels, meet(): pl.pallas_call(functools.partial(middle_kernel, (layers, wide, windows)),...  35.3 us
    pallas_call x1, Pallas kernels, finish(): pl.pallas_call(finish_kernel, out_shape=jax.ShapeDtypeStruct((count, pair...  2 us

profile of v7, /device:TPU:0, one launch (start us, length us, event | category | flops | bytes accessed | tf_op | source)
XLA Modules:
  0.0 37.3 jit_solution(12729270691406392634)
XLA Ops:
  0.0 35.3 %shard_map.55 = (bf16[256,2048]{1,0:T(8,128)(2,1)S(1)}, bf16[256,1024]{1,0:T(8,128)(2,1)S(1)}, bf16[1024,2048]{1,0:T(8,128)(2,1)S(1)}) custom-call(s32[16]{0:T(128)} %offsets_hbm.1, s32[32]{0:T(128)} %mask_hbm.1, bf16[256,3000]{1,0:T(8,128)(2,1)} %bitcast.3, bf16[4,3000,256]{2,1,0:T(8,128)(2,1)} %constant.4.clone.table_hbm, ...), custom_call_target="tpu_custom_call" | custom-call | tf_op jit(solution)/shard_map/pallas_call | solution.py:827
  35.3 2.0 %shard_map.56 = bf16[32,16,2048]{2,1,0:T(8,128)(2,1)} custom-call(bf16[32,8,2048]{2,1,0:T(8,128)(2,1)S(1)} %bitcast.2, bf16[256,1024]{1,0:T(8,128)(2,1)S(1)} %get-tuple-element.9.cross_ref, bf16[1024,2048]{1,0:T(8,128)(2,1)S(1)} %get-tuple-element.10.table_ref), custom_call_target="tpu_custom_call" | custom-call | tf_op jit(solution)/shard_map/pallas_call | solution.py:889

commit v8 on v7

--- a/solution.py
+++ b/solution.py
@@ -460,19 +460,13 @@
 
 
 def middle_kernel(shape, offsets_hbm, mask_hbm, records_hbm, table_hbm, inverse_hbm, half_ref, cross_ref, inverse,
-                  offsets_ref, mask_ref, records, table, crossed, spectrum, white, held, spec, made, back, joined,
+                  offsets_ref, mask_ref, records, table, crossed, spectrum, square, white, gains, column, held, spec, made, back, joined,
                   l_sem, x_send, f_send, g_send, s_recv, r_send, r_recv):
     layers, wide, windows = shape
     pairs = offsets_ref.shape[0]
     count = records.shape[0] // windows
     chunks, width = table.shape[0], table.shape[2]
-    load = [pltpu.make_async_copy(records_hbm, records, l_sem.at[chunks])]
-    for n in range(chunks):
-        load.append(pltpu.make_async_copy(table_hbm.at[n], table.at[n], l_sem.at[n]))
-    load.append(pltpu.make_async_copy(offsets_hbm, offsets_ref, l_sem.at[chunks + 1]))
-    load.append(pltpu.make_async_copy(mask_hbm, mask_ref, l_sem.at[chunks + 2]))
-    for one in load:
-        one.start()
+    rows = count * windows
     parts = layers * wide
     pitch = spec.shape[0] // (2 * windows)
     half, top, last = layers // 2, layers - 1, parts - 1
@@ -485,6 +479,23 @@
     mate_q = (q + 2) % wide
     far_q = (sib_q + 2) % wide
     near = c == 0
+
+    def nearest(j):
+        return jnp.where(j == 0, q, jnp.where(j == 1, sib_q, jnp.where(j == 2, mate_q, far_q)))
+
+    def chunk(j):
+        return pltpu.make_async_copy(table_hbm.at[nearest(j)], table.at[j], l_sem.at[j])
+
+    load = [
+        pltpu.make_async_copy(records_hbm, records, l_sem.at[chunks]),
+        pltpu.make_async_copy(offsets_hbm, offsets_ref, l_sem.at[chunks + 1]),
+        pltpu.make_async_copy(mask_hbm, mask_ref, l_sem.at[chunks + 2]),
+    ]
+    load[0].start()
+    for n in range(chunks):
+        chunk(n).start()
+    for one in load[1:]:
+        one.start()
     inner_low, inner_high = z == half - 1, z == half
     neighbour = jnp.where(
         jnp.logical_or(z == 0, jnp.logical_and(inner_low, c == 1)), me + wide, me - wide)
@@ -512,37 +523,6 @@
     replies_far = jnp.where(inner_low, wide, jnp.where(jnp.logical_and(inner_high, c == 1), 2 * wide - 1, 0))
     ships_there = jnp.where(jnp.logical_and(inner_low, near), 0, 1)
 
-    load[0].wait()
-    def transform(n, carry):
-        pltpu.make_async_copy(table_hbm.at[n], table.at[n], l_sem.at[n]).wait()
-        spectrum[n] = jnp.dot(records[...], table[n], preferred_element_type=jnp.float32)
-        return carry
-
-    lax.fori_loop(0, chunks, transform, 0)
-    for one in load[chunks + 1:]:
-        one.wait()
-    upper = lax.broadcasted_iota(jnp.int32, (2 * windows, 1), 0) < windows
-
-    def whitening(i, carry):
-        rows = pl.ds(pl.multiple_of(i * 2 * windows, 2 * windows), 2 * windows)
-        values = [
-            spectrum[x * LANES // width, rows, x * LANES % width:x * LANES % width + LANES]
-            for x in range(2 * wide)]
-        square = values[0] * values[0]
-        for value in values[1:]:
-            square += value * value
-        power = jnp.sum(square, axis=1, keepdims=True) * (1.0 / (2 * F))
-        alive = jnp.where(upper, mask_ref[2 * i].astype(jnp.float32), mask_ref[2 * i + 1].astype(jnp.float32))
-        gain = alive * lax.rsqrt(power + 1e-06)
-        for x, value in enumerate(values):
-            white[x, rows] = (value * gain).astype(jnp.bfloat16)
-        return carry
-
-    lax.fori_loop(0, count // 2, whitening, 0, unroll=4)
-    fetch = pltpu.make_async_copy(inverse_hbm, inverse, l_sem.at[0])
-    fetch.start()
-    pl.semaphore_wait(barrier, wide - 1 + replies_far + ships_there)
-
     def remote(source, target, send, recv, device):
         return pltpu.make_async_remote_copy(
             src_ref=source, dst_ref=target, send_sem=send, recv_sem=recv,
@@ -553,10 +533,10 @@
         return white.at[ri * wide + col]
 
     def swap(ri, col):
-        return remote(piece(ri, col), held.at[me, ri], x_send, s_recv.at[me], first + col)
+        return remote(piece(ri, col), held.at[me, pl.ds(ri * rows, rows)], x_send, s_recv.at[me], first + col)
 
     def ship_own(ri):
-        return remote(piece(ri, q), held.at[me, ri], f_send, s_recv.at[me], neighbour)
+        return remote(piece(ri, q), held.at[me, pl.ds(ri * rows, rows)], f_send, s_recv.at[me], neighbour)
 
     def ship(s):
         return remote(held.at[s], held.at[s], f_send, s_recv.at[s], neighbour)
@@ -564,7 +544,7 @@
     both_ways = jnp.logical_and(inner_low, c == 1)
 
     def drop_own(ri):
-        return remote(piece(ri, q), held.at[me, ri], g_send, s_recv.at[me], me - wide)
+        return remote(piece(ri, q), held.at[me, pl.ds(ri * rows, rows)], g_send, s_recv.at[me], me - wide)
 
     def drop(s):
         return remote(held.at[s], held.at[s], g_send, s_recv.at[s], me - wide)
@@ -578,28 +558,92 @@
     def shipped(slots, send):
         remote(held.at[0:slots], held.at[0:slots], send, s_recv.at[0], neighbour).wait_send()
 
-    for ri in range(2):
-        ship_own(ri).start()
-
-    @pl.when(both_ways)
-    def _():
-        for ri in range(2):
-            drop_own(ri).start()
-    columns = (sib_q, mate_q, far_q)
-    for col in columns:
-        for ri in range(2):
-            swap(ri, col).start()
-
-    def settle(s, load):
-        for ri in range(2):
-            def one(i, carry):
-                value = load(ri, i).astype(jnp.float32)
+    def gain_to(send, device):
+        return remote(gains, held.at[me, pl.ds(2 * rows, 16)], send, s_recv.at[me], device)
+
+    def clear(i, carry):
+        joined[pl.ds(pl.multiple_of(i * 64, 64), 64), :] = jnp.zeros((64, LANES), jnp.float32)
+        return carry
+
+    lax.fori_loop(0, joined.shape[0] // 64, clear, 0)
+
+    def blank(x, carry):
+        spec[pl.ds(pl.multiple_of(x * pitch + parts * count, 8), count), :] = jnp.zeros((count, LANES), jnp.float32)
+        return carry
+
+    lax.fori_loop(0, 2 * windows, blank, 0)
+    square[...] = jnp.zeros(square.shape, jnp.float32)
+    load[0].wait()
+
+    def transform(j, carry):
+        col = nearest(j)
+        chunk(j).wait()
+        spectrum[...] = jnp.dot(records[...], table[j], preferred_element_type=jnp.float32)
+
+        def narrow(i, inner):
+            some = pl.ds(pl.multiple_of(i * 16, 16), 16)
+            real, imag = spectrum[some, :LANES], spectrum[some, LANES:]
+            white[col, some] = real.astype(jnp.bfloat16)
+            white[wide + col, some] = imag.astype(jnp.bfloat16)
+            square[some, :] += real * real + imag * imag
+            return inner
+
+        lax.fori_loop(0, rows // 16, narrow, 0, unroll=4)
+
+        @pl.when(j == 0)
+        def _():
+            pl.semaphore_wait(barrier, wide - 1 + replies_far + ships_there)
+            for ri in range(2):
+                ship_own(ri).start()
+
+            @pl.when(both_ways)
+            def _():
+                for ri in range(2):
+                    drop_own(ri).start()
+
+        @pl.when(j > 0)
+        def _():
+            for ri in range(2):
+                swap(ri, col).start()
+        return carry
+
+    lax.fori_loop(0, chunks, transform, 0)
+    for one in load[1:]:
+        one.wait()
+    place = lax.broadcasted_iota(jnp.int32, (16, LANES), 0)
+    channel = lax.broadcasted_iota(jnp.int32, (8, LANES), 1) // windows
+    terms = jnp.zeros((16, LANES), jnp.float32)
+    for part in range(rows // LANES):
+        total = jnp.sum(square[part * LANES:(part + 1) * LANES, :], axis=1, keepdims=True)
+        scale = jnp.broadcast_to(lax.rsqrt(total * (1.0 / (2 * F)) + 1e-06), (LANES, LANES)).T[:8]
+        alive = jnp.zeros((8, LANES), jnp.float32)
+        for n in range(LANES // windows):
+            alive = jnp.where(channel == n, mask_ref[part * (LANES // windows) + n].astype(jnp.float32), alive)
+        rest = (scale * alive)[:1]
+        for term in range(3):
+            kept = rest.astype(jnp.bfloat16).astype(jnp.float32)
+            terms = jnp.where(place == part * 3 + term, kept, terms)
+            rest = rest - kept
+    gains[...] = terms.astype(jnp.bfloat16)
+    fetch = pltpu.make_async_copy(inverse_hbm, inverse, l_sem.at[0])
+    fetch.start()
+
+    def settle(s, gain, piece_of):
+        for part in range(rows // LANES):
+            scale = sum(gain[part * 3 + term:part * 3 + term + 1].astype(jnp.float32) for term in range(3))
+            column[part * LANES:(part + 1) * LANES, :] = jnp.broadcast_to(scale, (LANES, LANES)).T
+
+        def one(i, carry):
+            some = pl.ds(pl.multiple_of(i * 2 * windows, 2 * windows), 2 * windows)
+            factor = column[some, :]
+            for ri in range(2):
+                value = piece_of(ri, i).astype(jnp.float32) * factor
                 for part in range(2):
                     row = ri * windows * pitch + s * count + 2 * i + part
                     spec[pl.ds(row, windows, stride=pitch), :] = value[part * windows:(part + 1) * windows]
-                return carry
-
-            lax.fori_loop(0, count // 2, one, 0, unroll=4)
+            return carry
+
+        lax.fori_loop(0, count // 2, one, 0, unroll=4)
 
     def own_rows(ri, i):
         return white[ri * wide + q, pl.ds(pl.multiple_of(i * 2 * windows, 2 * windows), 2 * windows)]
@@ -614,7 +658,16 @@
             @pl.when(downward)
             def _():
                 drop(s).start()
-        settle(s, lambda ri, i: held[s, ri, pl.ds(pl.multiple_of(i * 2 * windows, 2 * windows), 2 * windows)])
+        settle(
+            s, held[s, 2 * rows:2 * rows + 16],
+            lambda ri, i: held[s, pl.ds(pl.multiple_of(ri * rows + i * 2 * windows, 2 * windows), 2 * windows)])
+
+    def takes(start, begin, end, onward=None, downward=None):
+        def one(j, carry):
+            take(start + nearest(j), onward, downward)
+            return carry
+
+        lax.fori_loop(begin, end, one, 0)
 
     def block(d, k):
         shift = offsets_ref[k]
@@ -651,77 +704,60 @@
         spans(*span, block)
         spans(*span, give)
 
-    for x in range(2 * windows):
-        spec[pl.ds(x * pitch + parts * count, count), :] = jnp.zeros((count, LANES), jnp.float32)
-
-    def clear(i, carry):
-        joined[pl.ds(pl.multiple_of(i * 64, 64), 64), :] = jnp.zeros((64, LANES), jnp.float32)
-        return carry
-
-    lax.fori_loop(0, joined.shape[0] // 64, clear, 0)
-
     y = q // 2
-    pair_1, pair_2 = (q, sib_q), (mate_q, far_q)
-
     def reached_1(start, more=0):
         return jnp.where(y == 0, start, start + 3), jnp.where(y == 0, start + 2, start + wide + more)
 
     def reached_2(start, more=0):
         return jnp.where(y == 0, start + 2, start), jnp.where(y == 0, start + wide + more, start + 3)
 
-    settle(me, own_rows)
-    for col in columns:
-        take(first + col, z >= 0, both_ways)
+    settle(me, gains[...], own_rows)
+    gain_to(f_send, neighbour).start()
+
+    @pl.when(both_ways)
+    def _():
+        gain_to(g_send, me - wide).start()
+    for col in (sib_q, mate_q, far_q):
+        gain_to(x_send, first + col).start()
+    takes(first, 1, wide, z >= 0, both_ways)
     blocks(first, first + wide, first + 1, first + wide + jnp.where(z == top, 1, 0))
 
     @pl.when(z == 0)
     def _():
-        for group, reached in ((pair_1, reached_1), (pair_2, reached_2)):
-            for col in group:
-                take(wide + col)
+        for begin, reached in ((0, reached_1), (2, reached_2)):
+            takes(wide, begin, begin + 2)
             blocks(0, wide, *reached(wide))
 
     @pl.when(inner_low)
     def _():
-        def lower(group):
-            for col in group:
-                take(col, jnp.logical_not(near))
-
-        lower(pair_1)
-        for col in pair_1:
-            take(base + col)
+        takes(0, 0, 2, jnp.logical_not(near))
+        takes(base, 0, 2)
         blocks(2 * y, 2 * y + 2, *reached_1(base))
         blocks(wide, base, *reached_1(base))
-        lower(pair_2)
+        takes(0, 2, wide, jnp.logical_not(near))
         blocks(2 - 2 * y, wide - 2 * y, *reached_1(base))
-        for col in pair_2:
-            take(base + col)
+        takes(base, 2, wide)
         blocks(0, base, *reached_2(base))
 
         @pl.when(near)
         def _():
-            for group, reached in ((pair_1, reached_1), (pair_2, reached_2)):
-                for col in group:
-                    take(top * wide + col)
+            for begin, reached in ((0, reached_1), (2, reached_2)):
+                takes(top * wide, begin, begin + 2)
                 blocks(0, base, *reached(top * wide, 1))
 
     @pl.when(inner_high)
     def _():
-        for group, reached in ((pair_1, reached_1), (pair_2, reached_2)):
-            for col in group:
-                take(top * wide + col, near)
+        for begin, reached in ((0, reached_1), (2, reached_2)):
+            takes(top * wide, begin, begin + 2, near)
             blocks(base, base + wide, *reached(top * wide, 1))
 
         @pl.when(jnp.logical_not(near))
         def _():
-            for col in pair_1 + pair_2:
-                take(wide + col)
+            takes(wide, 0, wide)
             spans(wide, base, top * wide, parts + 1, block)
-            for col in pair_1:
-                take(col)
+            takes(0, 0, 2)
             blocks(2 * y, 2 * y + 2, top * wide, parts + 1)
-            for col in pair_2:
-                take(col)
+            takes(0, 2, wide)
             blocks(2 - 2 * y, wide - 2 * y, top * wide, parts + 1)
             spans(wide, base, top * wide, parts + 1, give)
 
@@ -823,7 +859,8 @@
     rows = count * windows
     width = 2 * LANES
     chunks = 2 * F // width
-    table = np.ascontiguousarray(forward_table(length).reshape(length, chunks, width).transpose(1, 0, 2))
+    table = np.ascontiguousarray(
+        forward_table(length).reshape(length, 2, chunks, LANES).transpose(2, 0, 1, 3).reshape(chunks, length, width))
     return pl.pallas_call(
         functools.partial(middle_kernel, (layers, wide, windows)),
         out_shape=[
@@ -845,9 +882,12 @@
             pltpu.VMEM((rows, length), jnp.bfloat16),
             pltpu.VMEM((chunks, length, width), jnp.bfloat16),
             pltpu.VMEM((count * pairs // 2, 2 * F), jnp.bfloat16),
-            pltpu.VMEM((chunks, rows, width), jnp.float32),
+            pltpu.VMEM((rows, width), jnp.float32),
+            pltpu.VMEM((rows, LANES), jnp.float32),
             pltpu.VMEM((2 * wide, rows, LANES), jnp.bfloat16),
-            pltpu.VMEM((parts, 2, rows, LANES), jnp.bfloat16),
+            pltpu.VMEM((16, LANES), jnp.bfloat16),
+            pltpu.VMEM((rows, LANES), jnp.float32),
+            pltpu.VMEM((parts, 2 * rows + 16, LANES), jnp.bfloat16),
             pltpu.VMEM((2 * windows * pitch, LANES), jnp.float32),
             pltpu.VMEM((parts * pairs, 2, count, LANES), jnp.bfloat16),
             pltpu.VMEM((pairs, wide, 2, count, LANES), jnp.bfloat16),

time: 37.5 us -> 36.9 us (0.984)
  Pallas kernels: 37.3 us -> 36.8 us
    pallas_call x1, Pallas kernels: 35.3 us -> 34.8 us  [meet(): pl.pallas_call(functools.partial(middle_kernel, (layers, wide, windows)),...]
where the time goes in v8:
time: 36.9 us; the launch traced here: 36.8 us
  Pallas kernels  36.8 us (100%)
    pallas_call x1, Pallas kernels, meet(): pl.pallas_call(functools.partial(middle_kernel, (layers, wide, windows)),...  34.8 us
    pallas_call x1, Pallas kernels, finish(): pl.pallas_call(finish_kernel, out_shape=jax.ShapeDtypeStruct((count, pair...  2 us

profile of v8, /device:TPU:0, one launch (start us, length us, event | category | flops | bytes accessed | tf_op | source)
XLA Modules:
  0.0 36.8 jit_solution(7197961632567460769)
XLA Ops:
  0.0 34.8 %shard_map.55 = (bf16[256,2048]{1,0:T(8,128)(2,1)S(1)}, bf16[256,1024]{1,0:T(8,128)(2,1)S(1)}, bf16[1024,2048]{1,0:T(8,128)(2,1)S(1)}) custom-call(s32[16]{0:T(128)} %offsets_hbm.1, s32[32]{0:T(128)} %mask_hbm.1, bf16[256,3000]{1,0:T(8,128)(2,1)} %bitcast.3, bf16[4,3000,256]{2,1,0:T(8,128)(2,1)} %constant.4.clone.table_hbm, ...), custom_call_target="tpu_custom_call" | custom-call | tf_op jit(solution)/shard_map/pallas_call | solution.py:864
  34.8 2.0 %shard_map.56 = bf16[32,16,2048]{2,1,0:T(8,128)(2,1)} custom-call(bf16[32,8,2048]{2,1,0:T(8,128)(2,1)S(1)} %bitcast.2, bf16[256,1024]{1,0:T(8,128)(2,1)S(1)} %get-tuple-element.9.cross_ref, bf16[1024,2048]{1,0:T(8,128)(2,1)S(1)} %get-tuple-element.10.table_ref), custom_call_target="tpu_custom_call" | custom-call | tf_op jit(solution)/shard_map/pallas_call | solution.py:929

commit v9 on v8

--- a/solution.py
+++ b/solution.py
@@ -460,8 +460,8 @@
 
 
 def middle_kernel(shape, offsets_hbm, mask_hbm, records_hbm, table_hbm, inverse_hbm, half_ref, cross_ref, inverse,
-                  offsets_ref, mask_ref, records, table, crossed, spectrum, square, white, gains, column, held, spec, made, back, joined,
-                  l_sem, x_send, f_send, g_send, s_recv, r_send, r_recv):
+                  offsets_ref, mask_ref, records, table, crossed, spectrum, square, white, gains, column, scales, held, spec, made, back, joined,
+                  l_sem, x_send, f_send, g_send, n_send, n_recv, s_recv, r_send, r_recv):
     layers, wide, windows = shape
     pairs = offsets_ref.shape[0]
     count = records.shape[0] // windows
@@ -558,8 +558,11 @@
     def shipped(slots, send):
         remote(held.at[0:slots], held.at[0:slots], send, s_recv.at[0], neighbour).wait_send()
 
-    def gain_to(send, device):
-        return remote(gains, held.at[me, pl.ds(2 * rows, 16)], send, s_recv.at[me], device)
+    def gain_to(device):
+        return remote(gains, scales.at[me], n_send, n_recv.at[me], device)
+
+    def gain_on(s, device):
+        return remote(scales.at[s], scales.at[s], n_send, n_recv.at[s], device)
 
     def clear(i, carry):
         joined[pl.ds(pl.multiple_of(i * 64, 64), 64), :] = jnp.zeros((64, LANES), jnp.float32)
@@ -648,7 +651,7 @@
     def own_rows(ri, i):
         return white[ri * wide + q, pl.ds(pl.multiple_of(i * 2 * windows, 2 * windows), 2 * windows)]
 
-    def take(s, onward=None, downward=None):
+    def arrive(s, onward, downward):
         ship(s).wait_recv()
         if onward is not None:
             @pl.when(onward)
@@ -658,16 +661,32 @@
             @pl.when(downward)
             def _():
                 drop(s).start()
+
+    def unfold(s, onward, downward):
+        gain_on(s, me).wait_recv()
+        if onward is not None:
+            @pl.when(onward)
+            def _():
+                gain_on(s, neighbour).start()
+        if downward is not None:
+            @pl.when(downward)
+            def _():
+                gain_on(s, me - wide).start()
         settle(
-            s, held[s, 2 * rows:2 * rows + 16],
+            s, scales[s],
             lambda ri, i: held[s, pl.ds(pl.multiple_of(ri * rows + i * 2 * windows, 2 * windows), 2 * windows)])
 
     def takes(start, begin, end, onward=None, downward=None):
         def one(j, carry):
-            take(start + nearest(j), onward, downward)
+            arrive(start + nearest(j), onward, downward)
             return carry
 
+        def two(j, carry):
+            unfold(start + nearest(j), onward, downward)
+            return carry
+
         lax.fori_loop(begin, end, one, 0)
+        lax.fori_loop(begin, end, two, 0)
 
     def block(d, k):
         shift = offsets_ref[k]
@@ -712,14 +731,15 @@
         return jnp.where(y == 0, start + 2, start), jnp.where(y == 0, start + wide + more, start + 3)
 
     settle(me, gains[...], own_rows)
-    gain_to(f_send, neighbour).start()
+    gain_to(neighbour).start()
 
     @pl.when(both_ways)
     def _():
-        gain_to(g_send, me - wide).start()
+        gain_to(me - wide).start()
     for col in (sib_q, mate_q, far_q):
-        gain_to(x_send, first + col).start()
-    takes(first, 1, wide, z >= 0, both_ways)
+        gain_to(first + col).start()
+    takes(first, 1, 2, z >= 0, both_ways)
+    takes(first, 2, wide, z >= 0, both_ways)
     blocks(first, first + wide, first + 1, first + wide + jnp.where(z == top, 1, 0))
 
     @pl.when(z == 0)
@@ -810,31 +830,33 @@
     lax.fori_loop(0, jnp.minimum(group, parts - me), collect, 0)
     pack(0, crossed)
     fetch.wait()
-
-    def invert(n, carry):
-        span = pl.ds(pl.multiple_of(n * SPAN, SPAN), SPAN)
-        lagged = jnp.dot(crossed[...], inverse[:, span], preferred_element_type=jnp.float32)
-        half_ref[:, span] = (lagged * (1.0 / math.sqrt(F))).astype(jnp.bfloat16)
-        return carry
-
-    lax.fori_loop(0, LAGS // SPAN, invert, 0)
+    for n in range(0, LAGS, SPAN):
+        lagged = jnp.dot(crossed[...], inverse[:, n:n + SPAN], preferred_element_type=jnp.float32)
+        half_ref[:, n:n + SPAN] = (lagged * (1.0 / math.sqrt(F))).astype(jnp.bfloat16)
     lax.fori_loop(group, parts - me, collect, 0)
     pack(1, cross_ref)
 
     shipped(wide - 1, x_send)
     forwards = jnp.logical_or(both_ways, jnp.logical_and(inner_high, near))
 
-    @pl.when(forwards)
+    def told(slots):
+        remote(scales.at[0:slots], scales.at[0:slots], n_send, n_recv.at[0], me).wait_send()
+
+    @pl.when(both_ways)
+    def _():
+        shipped(wide, g_send)
+        shipped(2 * wide, f_send)
+        told(4 * wide - 1)
+
+    @pl.when(jnp.logical_and(inner_high, near))
     def _():
         shipped(2 * wide, f_send)
+        told(3 * wide - 1)
 
     @pl.when(jnp.logical_not(forwards))
     def _():
         shipped(wide, f_send)
-
-    @pl.when(both_ways)
-    def _():
-        shipped(wide, g_send)
+        told(2 * wide - 1)
 
     for i in range(parts):
         layer, odd = i // wide, i % 2 == 1
@@ -887,7 +909,8 @@
             pltpu.VMEM((2 * wide, rows, LANES), jnp.bfloat16),
             pltpu.VMEM((16, LANES), jnp.bfloat16),
             pltpu.VMEM((rows, LANES), jnp.float32),
-            pltpu.VMEM((parts, 2 * rows + 16, LANES), jnp.bfloat16),
+            pltpu.VMEM((parts, 16, LANES), jnp.bfloat16),
+            pltpu.VMEM((parts, 2 * rows, LANES), jnp.bfloat16),
             pltpu.VMEM((2 * windows * pitch, LANES), jnp.float32),
             pltpu.VMEM((parts * pairs, 2, count, LANES), jnp.bfloat16),
             pltpu.VMEM((pairs, wide, 2, count, LANES), jnp.bfloat16),
@@ -896,6 +919,8 @@
             pltpu.SemaphoreType.DMA,
             pltpu.SemaphoreType.DMA,
             pltpu.SemaphoreType.DMA,
+            pltpu.SemaphoreType.DMA,
+            pltpu.SemaphoreType.DMA((parts,)),
             pltpu.SemaphoreType.DMA((parts,)),
             pltpu.SemaphoreType.DMA,
             pltpu.SemaphoreType.DMA((pairs,)),

time: 36.9 us -> 36.9 us (level)
  no operation moved by 1% of the time
where the time goes in v9:
time: 36.9 us; the launch traced here: 36.7 us
  Pallas kernels  36.7 us (99%)
    pallas_call x1, Pallas kernels, meet(): pl.pallas_call(functools.partial(middle_kernel, (layers, wide, windows)),...  34.7 us
    pallas_call x1, Pallas kernels, finish(): pl.pallas_call(finish_kernel, out_shape=jax.ShapeDtypeStruct((count, pair...  2 us

profile of v9, /device:TPU:0, one launch (start us, length us, event | category | flops | bytes accessed | tf_op | source)
XLA Modules:
  0.0 36.7 jit_solution(15556580203135830412)
XLA Ops:
  0.0 34.7 %shard_map.55 = (bf16[256,2048]{1,0:T(8,128)(2,1)S(1)}, bf16[256,1024]{1,0:T(8,128)(2,1)S(1)}, bf16[1024,2048]{1,0:T(8,128)(2,1)S(1)}) custom-call(s32[16]{0:T(128)} %offsets_hbm.1, s32[32]{0:T(128)} %mask_hbm.1, bf16[256,3000]{1,0:T(8,128)(2,1)} %bitcast.3, bf16[4,3000,256]{2,1,0:T(8,128)(2,1)} %constant.4.clone.table_hbm, ...), custom_call_target="tpu_custom_call" | custom-call | tf_op jit(solution)/shard_map/pallas_call | solution.py:886
  34.7 2.0 %shard_map.56 = bf16[32,16,2048]{2,1,0:T(8,128)(2,1)} custom-call(bf16[32,8,2048]{2,1,0:T(8,128)(2,1)S(1)} %bitcast.2, bf16[256,1024]{1,0:T(8,128)(2,1)S(1)} %get-tuple-element.9.cross_ref, bf16[1024,2048]{1,0:T(8,128)(2,1)S(1)} %get-tuple-element.10.table_ref), custom_call_target="tpu_custom_call" | custom-call | tf_op jit(solution)/shard_map/pallas_call | solution.py:954

commit v10 on v9

--- a/solution.py
+++ b/solution.py
@@ -483,8 +483,11 @@
     def nearest(j):
         return jnp.where(j == 0, q, jnp.where(j == 1, sib_q, jnp.where(j == 2, mate_q, far_q)))
 
+    def slowest(j):
+        return jnp.where(j == 0, q, jnp.where(j == 1, mate_q, jnp.where(j == 2, sib_q, far_q)))
+
     def chunk(j):
-        return pltpu.make_async_copy(table_hbm.at[nearest(j)], table.at[j], l_sem.at[j])
+        return pltpu.make_async_copy(table_hbm.at[slowest(j)], table.at[j], l_sem.at[j])
 
     load = [
         pltpu.make_async_copy(records_hbm, records, l_sem.at[chunks]),
@@ -500,7 +503,8 @@
     neighbour = jnp.where(
         jnp.logical_or(z == 0, jnp.logical_and(inner_low, c == 1)), me + wide, me - wide)
     own_end = jnp.where(
-        z == 0, base, jnp.where(jnp.logical_and(inner_low, c == 1), base + wide, parts + 1))
+        z == 0, jnp.where(near, base, jnp.where(q < 2, wide + 2, wide)),
+        jnp.where(jnp.logical_and(inner_low, c == 1), base + wide, parts + 1))
     barrier = pltpu.get_barrier_semaphore()
 
     def greet(device, condition):
@@ -579,7 +583,7 @@
     load[0].wait()
 
     def transform(j, carry):
-        col = nearest(j)
+        col = slowest(j)
         chunk(j).wait()
         spectrum[...] = jnp.dot(records[...], table[j], preferred_element_type=jnp.float32)
 
@@ -651,38 +655,30 @@
     def own_rows(ri, i):
         return white[ri * wide + q, pl.ds(pl.multiple_of(i * 2 * windows, 2 * windows), 2 * windows)]
 
-    def arrive(s, onward, downward):
+    def arrive(s, onward):
         ship(s).wait_recv()
         if onward is not None:
             @pl.when(onward)
             def _():
                 ship(s).start()
-        if downward is not None:
-            @pl.when(downward)
-            def _():
-                drop(s).start()
-
-    def unfold(s, onward, downward):
+
+    def unfold(s, onward):
         gain_on(s, me).wait_recv()
         if onward is not None:
             @pl.when(onward)
             def _():
                 gain_on(s, neighbour).start()
-        if downward is not None:
-            @pl.when(downward)
-            def _():
-                gain_on(s, me - wide).start()
         settle(
             s, scales[s],
             lambda ri, i: held[s, pl.ds(pl.multiple_of(ri * rows + i * 2 * windows, 2 * windows), 2 * windows)])
 
-    def takes(start, begin, end, onward=None, downward=None):
+    def takes(start, begin, end, onward=None):
         def one(j, carry):
-            arrive(start + nearest(j), onward, downward)
+            arrive(start + nearest(j), onward)
             return carry
 
         def two(j, carry):
-            unfold(start + nearest(j), onward, downward)
+            unfold(start + nearest(j), onward)
             return carry
 
         lax.fori_loop(begin, end, one, 0)
@@ -719,9 +715,13 @@
         def _():
             reply(d, k).start()
 
-    def blocks(*span):
-        spans(*span, block)
-        spans(*span, give)
+    def blocks(d_begin, d_end, u_begin, u_end):
+        def reach(u, carry):
+            spans(d_begin, d_end, u, u + 1, block)
+            spans(d_begin, d_end, u, u + 1, give)
+            return carry
+
+        lax.fori_loop(u_begin, u_end, reach, 0)
 
     y = q // 2
     def reached_1(start, more=0):
@@ -732,29 +732,48 @@
 
     settle(me, gains[...], own_rows)
     gain_to(neighbour).start()
+    for col in (sib_q, mate_q, far_q):
+        gain_to(first + col).start()
+    arrive(first + sib_q, z >= 0)
 
     @pl.when(both_ways)
     def _():
+        drop(first + sib_q).start()
         gain_to(me - wide).start()
-    for col in (sib_q, mate_q, far_q):
-        gain_to(first + col).start()
-    takes(first, 1, 2, z >= 0, both_ways)
-    takes(first, 2, wide, z >= 0, both_ways)
+    unfold(first + sib_q, z >= 0)
+
+    @pl.when(both_ways)
+    def _():
+        gain_on(first + sib_q, me - wide).start()
+    takes(first, 2, wide, z >= 0)
     blocks(first, first + wide, first + 1, first + wide + jnp.where(z == top, 1, 0))
 
     @pl.when(z == 0)
     def _():
-        for begin, reached in ((0, reached_1), (2, reached_2)):
-            takes(wide, begin, begin + 2)
-            blocks(0, wide, *reached(wide))
+        takes(wide, 0, 2)
+        blocks(0, wide, *reached_1(wide))
+
+        @pl.when(near)
+        def _():
+            takes(wide, 2, wide)
+            blocks(0, wide, *reached_2(wide))
 
     @pl.when(inner_low)
     def _():
         takes(0, 0, 2, jnp.logical_not(near))
+
+        @pl.when(jnp.logical_not(near))
+        def _():
+            blocks(2 * y, 2 * y + 2, jnp.where(y == 0, wide + 2, wide + 1), jnp.where(y == 0, base, base - 1))
         takes(base, 0, 2)
         blocks(2 * y, 2 * y + 2, *reached_1(base))
         blocks(wide, base, *reached_1(base))
         takes(0, 2, wide, jnp.logical_not(near))
+
+        @pl.when(jnp.logical_not(near))
+        def _():
+            blocks(0, wide, wide, jnp.where(y == 0, wide, wide + 1))
+            blocks(2 - 2 * y, wide - 2 * y, jnp.where(y == 0, wide + 2, wide + 1), jnp.where(y == 0, base, base - 1))
         blocks(2 - 2 * y, wide - 2 * y, *reached_1(base))
         takes(base, 2, wide)
         blocks(0, base, *reached_2(base))
@@ -774,12 +793,13 @@
         @pl.when(jnp.logical_not(near))
         def _():
             takes(wide, 0, wide)
-            spans(wide, base, top * wide, parts + 1, block)
+            blocks(wide, base, *reached_1(top * wide, 1))
+            spans(wide, base, *reached_2(top * wide, 1), block)
             takes(0, 0, 2)
             blocks(2 * y, 2 * y + 2, top * wide, parts + 1)
             takes(0, 2, wide)
             blocks(2 - 2 * y, wide - 2 * y, top * wide, parts + 1)
-            spans(wide, base, top * wide, parts + 1, give)
+            spans(wide, base, *reached_2(top * wide, 1), give)
 
     group = pairs // 2
 
@@ -793,7 +813,9 @@
                     joined[pl.ds(row, 8, stride=group), :] = value[part * 8:part * 8 + 8]
 
     def collect(k, carry):
-        away = me + k + 1 >= own_end
+        u = me + k + 1
+        kept = jnp.logical_and(jnp.logical_and(z == 0, q == wide - 1), u == base - 1)
+        away = jnp.logical_and(u >= own_end, jnp.logical_not(kept))
         def received(cols):
             remote(back.at[k, 0:cols], back.at[k, 0:cols], r_send, r_recv.at[k], me).wait_recv()
 
@@ -837,20 +859,22 @@
     pack(1, cross_ref)
 
     shipped(wide - 1, x_send)
-    forwards = jnp.logical_or(both_ways, jnp.logical_and(inner_high, near))
+    forwards = jnp.logical_or(jnp.logical_and(inner_low, c == 1), jnp.logical_and(inner_high, near))
 
     def told(slots):
         remote(scales.at[0:slots], scales.at[0:slots], n_send, n_recv.at[0], me).wait_send()
 
+    @pl.when(forwards)
+    def _():
+        shipped(2 * wide, f_send)
+
     @pl.when(both_ways)
     def _():
-        shipped(wide, g_send)
-        shipped(2 * wide, f_send)
-        told(4 * wide - 1)
+        shipped(2, g_send)
+        told(3 * wide + 1)
 
     @pl.when(jnp.logical_and(inner_high, near))
     def _():
-        shipped(2 * wide, f_send)
         told(3 * wide - 1)
 
     @pl.when(jnp.logical_not(forwards))
@@ -858,14 +882,23 @@
         shipped(wide, f_send)
         told(2 * wide - 1)
 
+    def owners(z, q, u):
+        c, early = q % 2, u in ((wide, wide + 1) if q < 2 else (base - 1,))
+        layer = min(u, last) // wide
+        if z == 0:
+            return (0,) if layer == 0 or (layer == 1 and (c == 0 or early)) else ()
+        if z == half - 1:
+            if layer == 1:
+                return (1,) if c == 0 or early else (0, 1)
+            return (0, 1) if layer == half or (layer == top and c == 0) else ()
+        if z == half:
+            return (0, 1, half) if layer == top and c == 1 else (half,) if layer >= half else ()
+        return (top,) if layer == top else ()
+
     for i in range(parts):
-        layer, odd = i // wide, i % 2 == 1
-        ends = base if layer == 0 else base + wide if layer == half - 1 and odd else parts + 1
         replies = sum(
-            min(ends, d + pairs + 1) - d - 1 for d in range(layer * wide, (layer + 1) * wide) if d != i)
-        if layer == half - 1 or (layer == half and odd):
-            begins = base if layer == half - 1 else base + wide
-            replies += sum(min(ends, d + pairs + 1) - begins for d in range(layer * wide))
+            d // wide in owners(i // wide, i % wide, u) and d != i and 0 <= u - 1 - d < pairs
+            for u in range(1, parts + 1) for d in range(parts))
 
         @pl.when(me == i)
         def _():

time: 36.9 us -> 36.3 us (0.984)
  Pallas kernels: 36.7 us -> 36.2 us
    pallas_call x1, Pallas kernels: 34.7 us -> 34.2 us  [meet(): pl.pallas_call(functools.partial(middle_kernel, (layers, wide, windows)),...]
where the time goes in v10:
time: 36.3 us; the launch traced here: 36.2 us
  Pallas kernels  36.2 us (100%)
    pallas_call x1, Pallas kernels, meet(): pl.pallas_call(functools.partial(middle_kernel, (layers, wide, windows)),...  34.2 us
    pallas_call x1, Pallas kernels, finish(): pl.pallas_call(finish_kernel, out_shape=jax.ShapeDtypeStruct((count, pair...  2 us

profile of v10, /device:TPU:0, one launch (start us, length us, event | category | flops | bytes accessed | tf_op | source)
XLA Modules:
  0.0 36.2 jit_solution(17773025085665169195)
XLA Ops:
  0.0 34.2 %shard_map.55 = (bf16[256,2048]{1,0:T(8,128)(2,1)S(1)}, bf16[256,1024]{1,0:T(8,128)(2,1)S(1)}, bf16[1024,2048]{1,0:T(8,128)(2,1)S(1)}) custom-call(s32[16]{0:T(128)} %offsets_hbm.1, s32[32]{0:T(128)} %mask_hbm.1, bf16[256,3000]{1,0:T(8,128)(2,1)} %bitcast.3, bf16[4,3000,256]{2,1,0:T(8,128)(2,1)} %constant.4.clone.table_hbm, ...), custom_call_target="tpu_custom_call" | custom-call | tf_op jit(solution)/shard_map/pallas_call | solution.py:919
  34.2 2.0 %shard_map.56 = bf16[32,16,2048]{2,1,0:T(8,128)(2,1)} custom-call(bf16[32,8,2048]{2,1,0:T(8,128)(2,1)S(1)} %bitcast.2, bf16[256,1024]{1,0:T(8,128)(2,1)S(1)} %get-tuple-element.9.cross_ref, bf16[1024,2048]{1,0:T(8,128)(2,1)S(1)} %get-tuple-element.10.table_ref), custom_call_target="tpu_custom_call" | custom-call | tf_op jit(solution)/shard_map/pallas_call | solution.py:987

commit v11 on v10

--- a/solution.py
+++ b/solution.py
@@ -776,13 +776,15 @@
             blocks(2 - 2 * y, wide - 2 * y, jnp.where(y == 0, wide + 2, wide + 1), jnp.where(y == 0, base, base - 1))
         blocks(2 - 2 * y, wide - 2 * y, *reached_1(base))
         takes(base, 2, wide)
-        blocks(0, base, *reached_2(base))
+        blocks(0, wide, *reached_2(base))
+        blocks(wide, base, *reached_2(base))
 
         @pl.when(near)
         def _():
             for begin, reached in ((0, reached_1), (2, reached_2)):
                 takes(top * wide, begin, begin + 2)
-                blocks(0, base, *reached(top * wide, 1))
+                blocks(0, wide, *reached(top * wide, 1))
+                blocks(wide, base, *reached(top * wide, 1))
 
     @pl.when(inner_high)
     def _():

time: 36.3 us -> 36.3 us (level)
  no operation moved by 1% of the time
where the time goes in v11:
time: 36.3 us; the launch traced here: 36.2 us
  Pallas kernels  36.2 us (100%)
    pallas_call x1, Pallas kernels, meet(): pl.pallas_call(functools.partial(middle_kernel, (layers, wide, windows)),...  34.2 us
    pallas_call x1, Pallas kernels, finish(): pl.pallas_call(finish_kernel, out_shape=jax.ShapeDtypeStruct((count, pair...  2 us

profile of v11, /device:TPU:0, one launch (start us, length us, event | category | flops | bytes accessed | tf_op | source)
XLA Modules:
  0.0 36.2 jit_solution(14033337531427260183)
XLA Ops:
  0.0 34.2 %shard_map.55 = (bf16[256,2048]{1,0:T(8,128)(2,1)S(1)}, bf16[256,1024]{1,0:T(8,128)(2,1)S(1)}, bf16[1024,2048]{1,0:T(8,128)(2,1)S(1)}) custom-call(s32[16]{0:T(128)} %offsets_hbm.1, s32[32]{0:T(128)} %mask_hbm.1, bf16[256,3000]{1,0:T(8,128)(2,1)} %bitcast.3, bf16[4,3000,256]{2,1,0:T(8,128)(2,1)} %constant.4.clone.table_hbm, ...), custom_call_target="tpu_custom_call" | custom-call | tf_op jit(solution)/shard_map/pallas_call | solution.py:921
  34.2 2.0 %shard_map.56 = bf16[32,16,2048]{2,1,0:T(8,128)(2,1)} custom-call(bf16[32,8,2048]{2,1,0:T(8,128)(2,1)S(1)} %bitcast.2, bf16[256,1024]{1,0:T(8,128)(2,1)S(1)} %get-tuple-element.9.cross_ref, bf16[1024,2048]{1,0:T(8,128)(2,1)S(1)} %get-tuple-element.10.table_ref), custom_call_target="tpu_custom_call" | custom-call | tf_op jit(solution)/shard_map/pallas_call | solution.py:989

commit v12 on v11

--- a/solution.py
+++ b/solution.py
@@ -767,7 +767,6 @@
             blocks(2 * y, 2 * y + 2, jnp.where(y == 0, wide + 2, wide + 1), jnp.where(y == 0, base, base - 1))
         takes(base, 0, 2)
         blocks(2 * y, 2 * y + 2, *reached_1(base))
-        blocks(wide, base, *reached_1(base))
         takes(0, 2, wide, jnp.logical_not(near))
 
         @pl.when(jnp.logical_not(near))
@@ -775,6 +774,7 @@
             blocks(0, wide, wide, jnp.where(y == 0, wide, wide + 1))
             blocks(2 - 2 * y, wide - 2 * y, jnp.where(y == 0, wide + 2, wide + 1), jnp.where(y == 0, base, base - 1))
         blocks(2 - 2 * y, wide - 2 * y, *reached_1(base))
+        blocks(wide, base, *reached_1(base))
         takes(base, 2, wide)
         blocks(0, wide, *reached_2(base))
         blocks(wide, base, *reached_2(base))

time: 36.3 us -> 36.3 us (level)
  no operation moved by 1% of the time
where the time goes in v12:
time: 36.3 us; the launch traced here: 36.2 us
  Pallas kernels  36.2 us (100%)
    pallas_call x1, Pallas kernels, meet(): pl.pallas_call(functools.partial(middle_kernel, (layers, wide, windows)),...  34.2 us
    pallas_call x1, Pallas kernels, finish(): pl.pallas_call(finish_kernel, out_shape=jax.ShapeDtypeStruct((count, pair...  2 us

profile of v12, /device:TPU:0, one launch (start us, length us, event | category | flops | bytes accessed | tf_op | source)
XLA Modules:
  0.0 36.2 jit_solution(8921467628828960967)
XLA Ops:
  0.0 34.2 %shard_map.55 = (bf16[256,2048]{1,0:T(8,128)(2,1)S(1)}, bf16[256,1024]{1,0:T(8,128)(2,1)S(1)}, bf16[1024,2048]{1,0:T(8,128)(2,1)S(1)}) custom-call(s32[16]{0:T(128)} %offsets_hbm.1, s32[32]{0:T(128)} %mask_hbm.1, bf16[256,3000]{1,0:T(8,128)(2,1)} %bitcast.3, bf16[4,3000,256]{2,1,0:T(8,128)(2,1)} %constant.4.clone.table_hbm, ...), custom_call_target="tpu_custom_call" | custom-call | tf_op jit(solution)/shard_map/pallas_call | solution.py:921
  34.2 2.0 %shard_map.56 = bf16[32,16,2048]{2,1,0:T(8,128)(2,1)} custom-call(bf16[32,8,2048]{2,1,0:T(8,128)(2,1)S(1)} %bitcast.2, bf16[256,1024]{1,0:T(8,128)(2,1)S(1)} %get-tuple-element.9.cross_ref, bf16[1024,2048]{1,0:T(8,128)(2,1)S(1)} %get-tuple-element.10.table_ref), custom_call_target="tpu_custom_call" | custom-call | tf_op jit(solution)/shard_map/pallas_call | solution.py:989
